TPU v7x, 32 devices: a whole 2x2x4 slice. The times are simulated.
32 devices in a mesh: dp: 16 (over z, y, x), tensor: 2 (over core).
Axes of the slice: x: 2, y: 2, z: 4, core: 2. Of those that a mesh axis runs over, the one named last changes fastest.
Arguments:
- tokens: bfloat16 [16, 2048, 512], P('dp', 'tensor'), may hold values from -6 to 6
- cotangent: bfloat16 [16, 2048, 512], P('dp', 'tensor'), may hold values from -6 to 6
- span_ids: int32 [16, 8, 256], P('dp'), may hold values from 0 to 1, never falling along the last dimension, each value on 1 to 192 neighbouring positions
- gain_one: float32 [512], replicated, may hold values from 0.25 to 1.75
- w_qkv: bfloat16 [512, 3, 512], P('dp', None, 'tensor'), may hold values from -0.25 to 0.25
- w_out: bfloat16 [512, 512], P('tensor', 'dp'), may hold values from -1 to 1
- b_out: float32 [512], replicated, may hold values from -3 to 3
- gain_two: float32 [512], replicated, may hold values from 0.25 to 1.75
- w_up: bfloat16 [512, 2048], P('dp', 'tensor'), may hold values from -0.25 to 0.25
- b_up: float32 [2048], P('tensor'), may hold values from -3 to 3
- w_down: bfloat16 [2048, 512], P('tensor', 'dp'), may hold values from -0.125 to 0.125
- b_down: float32 [512], replicated, may hold values from -3 to 3
Outputs:
- result: bfloat16 [16, 2048, 512], P('dp', 'tensor')
- d_tokens: bfloat16 [16, 2048, 512], P('dp', 'tensor')
- d_gain_one: float32 [512], replicated
- d_w_qkv: float32 [512, 3, 512], P('dp', None, 'tensor')
- d_w_out: float32 [512, 512], P('tensor', 'dp')
- d_b_out: float32 [512], replicated
- d_gain_two: float32 [512], replicated
- d_w_up: float32 [512, 2048], P('dp', 'tensor')
- d_b_up: float32 [2048], replicated
- d_w_down: float32 [2048, 512], P('tensor', 'dp')
- d_b_down: float32 [512], replicated
Inputs may be any that keep to these rules, and one draw needn't show every extreme that they name: `span_ids`: within each block of 256 positions the span numbers never fall and each of the 2 spans holds 1 to 192 positions.
All inputs are finite; a program needn't handle non-finite values.
Results may differ from a plain program's by a relative error of at most 0.014.
Values may be sent and summed in bfloat16 or wider, within the bound.
A program may use at most 128 MiB of HBM per device.

v0:
```python
import math

import jax
import jax.numpy as jnp
from jax import lax
from jax.sharding import PartitionSpec as P

HD = 64
BLK = 256
SPB = 2


epsilon = 1e-05
masked = -1e30


def normalize(values, gain_vec):
    centre = values - jnp.mean(values, axis=-1, keepdims=True)
    spread = jnp.mean(centre * centre, axis=-1, keepdims=True)
    inverse = lax.rsqrt(spread + epsilon)
    unit_rows = centre * inverse
    return (unit_rows, inverse, unit_rows * gain_vec)


def normalize_back(incoming_grad, unit_rows, inverse, gain_vec):
    scaled = incoming_grad * gain_vec
    mean_one = jnp.mean(scaled, axis=-1, keepdims=True)
    mean_two = jnp.mean(scaled * unit_rows, axis=-1, keepdims=True)
    return (
        inverse * (scaled - mean_one - unit_rows * mean_two),
        jnp.sum(incoming_grad * unit_rows, axis=0),
    )


def pair_rows(values):
    return lax.all_gather(values, "tensor", axis=0, tiled=True)


def pair_sums(term_fn, rows):
    return lax.psum_scatter(
        term_fn(jnp.int32(0), rows * lax.axis_size("tensor")).astype(jnp.bfloat16),
        "tensor",
        scatter_dimension=0,
        tiled=True,
    ).astype(jnp.float32)


def scores(queries, key_rows, key_sum, counts_all, allowed):
    scaling = 1.0 / math.sqrt(queries.shape[-1])
    near_scores = (
        jnp.einsum("bie,bje->bij", queries, key_rows, preferred_element_type=jnp.float32) * scaling
    )
    far_scores = (
        jnp.einsum("bie,ce->bic", queries, key_sum, preferred_element_type=jnp.float32) * scaling
    )
    far_scores = far_scores + jnp.log(counts_all).reshape(-1)
    far_scores = jnp.where(allowed[:, None, :], far_scores, masked)
    return (near_scores, far_scores)


def span_means(key_rows, value_rows, member_low, counts):
    head_size = key_rows.shape[-1]
    key_sum = jnp.einsum("bjm,bje->bme", member_low, key_rows, preferred_element_type=jnp.float32)
    value_sum = jnp.einsum(
        "bjm,bje->bme", member_low, value_rows, preferred_element_type=jnp.float32
    )
    key_sum = (key_sum / counts[:, :, None]).astype(jnp.bfloat16).reshape(-1, head_size)
    value_sum = (value_sum / counts[:, :, None]).astype(jnp.bfloat16).reshape(-1, head_size)
    return (key_sum, value_sum)


def attend(queries, key_rows, value_rows, key_sum, value_sum, counts_all, allowed):
    near_scores, far_scores = scores(queries, key_rows, key_sum, counts_all, allowed)
    largest = jnp.maximum(jnp.max(near_scores, axis=-1), jnp.max(far_scores, axis=-1))
    near_exp = jnp.exp(near_scores - largest[..., None])
    far_exp = jnp.exp(far_scores - largest[..., None])
    denominator = jnp.sum(near_exp, axis=-1) + jnp.sum(far_exp, axis=-1)
    near_prob = (near_exp / denominator[..., None]).astype(jnp.bfloat16)
    far_prob = (far_exp / denominator[..., None]).astype(jnp.bfloat16)
    attended = jnp.einsum("bij,bje->bie", near_prob, value_rows, preferred_element_type=jnp.float32)
    attended = attended + jnp.einsum(
        "bic,ce->bie", far_prob, value_sum, preferred_element_type=jnp.float32
    )
    return (attended.astype(jnp.bfloat16), largest + jnp.log(denominator))


def head_backward(
    queries, key_rows, value_rows, grad_heads, log_total, key_sum, value_sum, counts_all, allowed
):
    scaling = 1.0 / math.sqrt(queries.shape[-1])
    near_scores, far_scores = scores(queries, key_rows, key_sum, counts_all, allowed)
    near_prob = jnp.exp(near_scores - log_total[..., None])
    far_prob = jnp.exp(far_scores - log_total[..., None])
    grad_value = jnp.einsum(
        "bij,bie->bje",
        near_prob.astype(jnp.bfloat16),
        grad_heads,
        preferred_element_type=jnp.float32,
    )
    grad_vsum = jnp.einsum(
        "bic,bie->ce", far_prob.astype(jnp.bfloat16), grad_heads, preferred_element_type=jnp.float32
    )
    near_dprob = jnp.einsum(
        "bie,bje->bij", grad_heads, value_rows, preferred_element_type=jnp.float32
    )
    far_dprob = jnp.einsum("bie,ce->bic", grad_heads, value_sum, preferred_element_type=jnp.float32)
    correction = jnp.sum(near_prob * near_dprob, axis=-1) + jnp.sum(far_prob * far_dprob, axis=-1)
    near_grad = (near_prob * (near_dprob - correction[..., None])).astype(jnp.bfloat16)
    far_grad = (far_prob * (far_dprob - correction[..., None])).astype(jnp.bfloat16)
    grad_query = jnp.einsum("bij,bje->bie", near_grad, key_rows, preferred_element_type=jnp.float32)
    grad_query = (
        grad_query
        + jnp.einsum("bic,ce->bie", far_grad, key_sum, preferred_element_type=jnp.float32)
    ) * scaling
    grad_key = (
        jnp.einsum("bij,bie->bje", near_grad, queries, preferred_element_type=jnp.float32) * scaling
    )
    grad_ksum = (
        jnp.einsum("bic,bie->ce", far_grad, queries, preferred_element_type=jnp.float32) * scaling
    )
    return (grad_query.astype(jnp.bfloat16), grad_key, grad_value, grad_ksum, grad_vsum)


def shards(
    tokens, cotangent, span_ids, gain_one, w_qkv, w_out, b_out, gain_two, w_up, b_up, w_down, b_down
):
    incoming = tokens[0].astype(jnp.float32)
    row_count = incoming.shape[0]
    full_qkv, full_out, full_up, full_down = (
        lax.all_gather(w_qkv, "dp", axis=0, tiled=True),
        lax.all_gather(w_out, "dp", axis=1, tiled=True),
        lax.all_gather(w_up, "dp", axis=0, tiled=True),
        lax.all_gather(w_down, "dp", axis=1, tiled=True),
    )
    unit_one, inverse_one, normed = normalize(incoming, gain_one)
    normed_low = normed.astype(jnp.bfloat16)
    span_all = span_ids[0]
    member_all = (span_all[:, :, None] == jnp.arange(SPB, dtype=jnp.int32)[None, None, :]).astype(
        jnp.float32
    )
    counts_all = jnp.sum(member_all, axis=1)
    total_blocks = span_all.shape[0]
    qkv_whole, out_whole, up_whole, down_whole, bias_whole = (
        full_qkv,
        full_out,
        full_up,
        full_down,
        b_up,
    )
    rows_one = pair_rows(normed_low)
    width = qkv_whole.shape[0]
    qkv_flat = qkv_whole.reshape(width, -1)
    length = rows_one.shape[0]
    blocks = length // BLK
    heads_here = qkv_whole.shape[2] // HD
    projected = jnp.dot(rows_one, qkv_flat, preferred_element_type=jnp.float32).astype(jnp.bfloat16)
    per_head = jnp.moveaxis(projected.reshape(blocks, BLK, 3, heads_here, HD), (2, 3), (0, 1))
    member_low = member_all.astype(jnp.bfloat16)
    allowed = jnp.arange(blocks)[:, None] > (jnp.arange(total_blocks * SPB) // SPB)[None, :]
    key_sums, value_sums = lax.map(
        lambda pieces: span_means(pieces[0], pieces[1], member_low, counts_all),
        (per_head[1], per_head[2]),
    )

    def forward_head(pieces):
        return attend(pieces[0], pieces[1], pieces[2], pieces[3], pieces[4], counts_all, allowed)

    attended, log_total = lax.map(
        forward_head, (per_head[0], per_head[1], per_head[2], key_sums, value_sums)
    )
    attended_flat = jnp.moveaxis(attended, 0, 2).reshape(length, -1)

    def project_attn(offset, amount):
        return jnp.dot(attended_flat, out_whole, preferred_element_type=jnp.float32)

    attn_total = pair_sums(project_attn, row_count)
    middle = incoming + (attn_total + b_out)
    unit_two, inverse_two, normed_two = normalize(middle, gain_two)
    rows_two = pair_rows(normed_two.astype(jnp.bfloat16))
    before_gelu = jnp.dot(rows_two, up_whole, preferred_element_type=jnp.float32) + bias_whole
    activated, gelu_pull = jax.vjp(jax.nn.gelu, before_gelu)
    hidden = activated.astype(jnp.bfloat16)

    def project_mlp(offset, amount):
        return jnp.dot(hidden, down_whole, preferred_element_type=jnp.float32)

    mlp_total = pair_sums(project_mlp, row_count)
    output = middle + (mlp_total + b_down)
    grad_rows = cotangent[0]
    grad_output = grad_rows.astype(jnp.float32)
    full_grad = pair_rows(grad_rows)
    grad_down = jnp.einsum("sf,sd->fd", hidden, full_grad, preferred_element_type=jnp.float32)
    grad_hidden = jnp.einsum("sd,fd->sf", full_grad, down_whole, preferred_element_type=jnp.float32)
    grad_inner = gelu_pull(grad_hidden)[0].astype(jnp.bfloat16)
    bias_up = jnp.sum(grad_inner, axis=0, dtype=jnp.float32)
    grad_up = jnp.einsum("sd,sf->df", rows_two, grad_inner, preferred_element_type=jnp.float32)

    def back_mlp_rows(offset, amount):
        return jnp.einsum("sf,df->sd", grad_inner, up_whole, preferred_element_type=jnp.float32)

    grad_second = pair_sums(back_mlp_rows, row_count)
    grad_norm_two, gain_two_part = normalize_back(grad_second, unit_two, inverse_two, gain_two)
    grad_mid = grad_output + grad_norm_two
    grad_branch = grad_mid.astype(jnp.bfloat16)
    full_branch = pair_rows(grad_branch)
    grad_wout = jnp.einsum(
        "sh,sd->hd", attended_flat, full_branch, preferred_element_type=jnp.float32
    )
    grad_attended = jnp.einsum(
        "sd,hd->sh", full_branch, out_whole, preferred_element_type=jnp.float32
    ).astype(jnp.bfloat16)
    grad_heads = jnp.moveaxis(grad_attended.reshape(blocks, BLK, heads_here, HD), 2, 0)

    def backward_head(pieces):
        return head_backward(
            pieces[0],
            pieces[1],
            pieces[2],
            pieces[3],
            pieces[4],
            pieces[5],
            pieces[6],
            counts_all,
            allowed,
        )

    grad_query, grad_key, grad_value, grad_ksums, grad_vsums = lax.map(
        backward_head,
        (per_head[0], per_head[1], per_head[2], grad_heads, log_total, key_sums, value_sums),
    )
    share_key = grad_ksums.reshape(heads_here, blocks, SPB, HD) / counts_all[None, :, :, None]
    share_value = grad_vsums.reshape(heads_here, blocks, SPB, HD) / counts_all[None, :, :, None]
    grad_key = (grad_key + jnp.einsum("bjm,hbme->hbje", member_all, share_key)).astype(jnp.bfloat16)
    grad_value = (grad_value + jnp.einsum("bjm,hbme->hbje", member_all, share_value)).astype(
        jnp.bfloat16
    )
    grad_projected = jnp.moveaxis(
        jnp.stack((grad_query, grad_key, grad_value), axis=0), (0, 1), (2, 3)
    ).reshape(length, -1)
    grad_qkv = jnp.einsum(
        "sd,sc->dc", rows_one, grad_projected, preferred_element_type=jnp.float32
    ).reshape(qkv_whole.shape)

    def back_attn_rows(offset, amount):
        return jnp.einsum("sc,dc->sd", grad_projected, qkv_flat, preferred_element_type=jnp.float32)

    grad_first = pair_sums(back_attn_rows, row_count)
    grad_norm_one, gain_one_part = normalize_back(grad_first, unit_one, inverse_one, gain_one)
    grad_input = grad_mid + grad_norm_one
    half_width = bias_up.shape[0]
    bias_up_full = lax.dynamic_update_slice(
        jnp.zeros((half_width * lax.axis_size("tensor"),), jnp.float32),
        bias_up,
        (lax.axis_index("tensor") * half_width,),
    )
    totals = lax.psum(
        (
            gain_one_part,
            gain_two_part,
            jnp.sum(grad_branch, axis=0, dtype=jnp.float32),
            jnp.sum(grad_output, axis=0),
            bias_up_full,
        ),
        ("dp", "tensor"),
    )
    grad_qkv, grad_wout, grad_up, grad_down = (
        lax.psum_scatter(grad_qkv, "dp", scatter_dimension=0, tiled=True),
        lax.psum_scatter(grad_wout, "dp", scatter_dimension=1, tiled=True),
        lax.psum_scatter(grad_up, "dp", scatter_dimension=0, tiled=True),
        lax.psum_scatter(grad_down, "dp", scatter_dimension=1, tiled=True),
    )
    factor = 1.0 / math.sqrt(lax.axis_size("dp") * lax.axis_size("tensor") * row_count)
    return (
        output.astype(jnp.bfloat16)[None],
        grad_input.astype(jnp.bfloat16)[None],
        totals[0] * factor,
        grad_qkv * factor,
        grad_wout * factor,
        totals[2] * factor,
        totals[1] * factor,
        grad_up * factor,
        totals[4] * factor,
        grad_down * factor,
        totals[3] * factor,
    )


def solution(mesh):
    in_specs = (
        P("dp", "tensor", None),
        P("dp", "tensor", None),
        P("dp", None, None),
        P(),
        P("dp", None, "tensor"),
        P("tensor", "dp"),
        P(),
        P(),
        P("dp", "tensor"),
        P("tensor"),
        P("tensor", "dp"),
        P(),
    )
    out_specs = (
        P("dp", "tensor", None),
        P("dp", "tensor", None),
        P(),
        P("dp", None, "tensor"),
        P("tensor", "dp"),
        P(),
        P(),
        P("dp", "tensor"),
        P(),
        P("tensor", "dp"),
        P(),
    )
    return jax.shard_map(shards, mesh=mesh, in_specs=in_specs, out_specs=out_specs, check_vma=False)
```

profile of v0, /device:TPU:0, one launch (start us, length us, event | category | flops | bytes accessed | tf_op | source)
XLA Modules:
  0.0 713.2 jit_solution(7615604891802510770)
XLA Ops:
  13.1 47.0 %all_gather.25 = bf16[512,3,256]{2,0,1:T(8,128)(2,1)S(1)} all-gather(bf16[32,3,256]{2,0,1:T(8,128)(2,1)S(1)} %copy-done.14), channel_id=1, replica_groups=mesh['dp'=16,'tensor'=2] {'dp'}, dimensions={0}, use_global_device_ids=true | all-gather | bytes 835584 | tf_op jit(solution)/shard_map/all_gather | solution.py:130
  60.4 36.9 %all_gather.26 = bf16[256,512]{0,1:T(8,128)(2,1)S(1)} all-gather(bf16[256,32]{0,1:T(8,128)(2,1)S(1)} %copy-done.18), channel_id=1, replica_groups=mesh['dp'=16,'tensor'=2] {'dp'}, dimensions={1}, use_global_device_ids=true | all-gather | bytes 278528 | tf_op jit(solution)/shard_map/all_gather | solution.py:131
  97.3 5.1 convolution_convert_fusion
  102.4 4.7 copy.64
  107.1 3.0 copy.111
  115.9 14.6 %while.50 = (s32[]{:T(128)}, bf16[4,8,256,64]{2,3,1,0:T(8,128)(2,1)}, f32[4,8,256]{2,1,0:T(8,128)S(1)}, bf16[4,8,256,64]{2,3,1,0:T(8,128)(2,1)S(1)}, bf16[4,8,25...) while((s32[]{:T(128)}, ...), condition=%wide.region_10.11_spmd.clone, body=%wide.region_5.10_spmd.clone.sunk | while | flops 147880064 | bytes 9204541 | solution.py:168
  136.7 6.9 reduce-scatter.9.cloned.1.call-done
  149.2 43.8 %all-gather.12.cloned.1.call-done = bf16[512,1024]{1,0:T(8,128)(2,1)} async-done(((bf16[32,1024]{1,0:T(8,128)(2,1)}), bf16[512,1024]{1,0:T(8,128)(2,1)}) %all-gather.12.cloned.1.call-update) | async-done | bytes 1048592 | tf_op jit(solution)/shard_map/all_gather | solution.py:132
  192.9 11.4 %all-gather.10.cloned.1.call-done = bf16[2048,512]{1,0:T(8,128)(2,1)} async-done(((bf16[1024,512]{1,0:T(8,128)(2,1)}), bf16[2048,512]{1,0:T(8,128)(2,1)}) %all-gather.10.cloned.1.call-update) | async-done | bytes 2097168 | tf_op jit(solution)/shard_map/all_gather | solution.py:36
  204.3 10.5 %multiply_convert_fusion.2 = (bf16[2048,1024]{1,0:T(8,128)(2,1)}, f32[2048,1024]{1,0:T(8,128)}) fusion(f32[1024]{0:T(1024)S(1)} %copy-done.22, bf16[2048,512]{1,0:T(8,128)(2,1)} %all-gather.10.cloned.1.call-done, bf16[512,1024]{1,0:T(8,128)(2,1)} %all-gather.12.cloned.1.call-done), kind=kOutput, calls=%fused_computation.129 | convolution fusion | flops 2168455168 | bytes 15732736 | tf_op jit(solution)/shard_map/dot_general | solution.py:180
  214.8 49.1 %all-gather.14.cloned.1.call-done = bf16[1024,512]{0,1:T(8,128)(2,1)} async-done(((bf16[1024,32]{0,1:T(8,128)(2,1)}), bf16[1024,512]{0,1:T(8,128)(2,1)}) %all-gather.14.cloned.1.call-update) | async-done | bytes 1048592 | tf_op jit(solution)/shard_map/all_gather | solution.py:133
  263.9 11.0 %all-gather.18.cloned.1.call-done = bf16[1,2048,512]{2,1,0:T(8,128)(2,1)} async-done(((bf16[1,1024,512]{2,1,0:T(8,128)(2,1)}), bf16[1,2048,512]{2,1,0:T(8,128)(2,1)}) %all-gather.18.cloned.1.call-update) | async-done | bytes 2097168 | tf_op jit(solution)/shard_map/all_gather | solution.py:36
  274.9 10.2 %convert_reduce_fusion = (f32[1024]{0:T(1024)S(1)}, bf16[2048,1024]{1,0:T(8,128)(2,1)S(1)}) fusion(f32[2048,1024]{1,0:T(8,128)} %get-tuple-element.582, f32[1024]{0:T(1024)S(1)} %copy-done.22, bf16[1024,512]{0,1:T(8,128)(2,1)} %all-gather.14.cloned.1.call-done, bf16[1,2048,512]{2,1,0:T(8,128)(2,1)} %all-gather.18.cloned.1.call-done), kind=kOutput, calls=%fused_computation.128 | convolution fusion | flops 2195717120 | bytes 15736832 | tf_op jit(solution)/shard_map/sd,fd->sf/dot_general | solution.py:193
  287.0 3.8 convolution_convert_fusion.1
  291.3 6.2 convolution_convert_fusion.2
  297.6 4.2 reduce-scatter.13.cloned.1.call-done
  304.7 10.0 %reduce-scatter.11.cloned.1.call-done = bf16[1024,512]{1,0:T(8,128)(2,1)} async-done(((bf16[2048,512]{1,0:T(8,128)(2,1)}), bf16[1024,512]{1,0:T(8,128)(2,1)}) %reduce-scatter.11.cloned.1.call-update) | async-done | bytes 1048592 | tf_op jit(solution)/shard_map/reduce_scatter | solution.py:40
  314.7 4.2 convert_reduce_fusion.3
  319.0 6.6 fusion.131
  325.7 7.2 %fusion.155 = f32[512,1024]{1,0:T(8,128)} fusion(bf16[2048,512]{1,0:T(8,128)(2,1)} %all-gather.10.cloned.1.call-done, bf16[2048,1024]{1,0:T(8,128)(2,1)} %copy-done.25), kind=kOutput, calls=%fused_computation.228 | convolution fusion | flops 2147483648 | bytes 8388608 | tf_op jit(solution)/shard_map/sd,sf->df/dot_general | solution.py:196
  333.1 3.3 convolution_convert_fusion.5
  341.3 32.6 %while.51 = (s32[]{:T(128)}, bf16[4,8,256,64]{2,3,0,1:T(8,128)(2,1)}, f32[4,8,256,64]{2,3,0,1:T(8,128)}, f32[4,8,256,64]{2,3,0,1:T(8,128)}, f32[4,16,64]{2,1,0:T...) while((s32[]{:T(128)}, ...), condition=%wide.region_21.22_spmd.clone, body=%wide.region_18.21_spmd.clone.sunk | while | flops 361561216 | bytes 22604664 | solution.py:227
  373.9 3.6 fusion.154
  387.4 3.0 fusion.127
  390.8 5.0 convolution_convert_fusion.4
  397.5 17.5 %reduce-scatter.23.cloned.1.call-done = f32[1024,32]{0,1:T(8,128)} async-done(((f32[1024,512]{0,1:T(8,128)}), f32[1024,32]{0,1:T(8,128)}) %reduce-scatter.23.cloned.1.call-update) | async-done | bytes 131088 | tf_op jit(solution)/shard_map/reduce_scatter | solution.py:270
  416.6 77.7 %reduce-scatter.21.cloned.1.call-done = f32[32,1024]{1,0:T(8,128)} async-done(((f32[512,1024]{1,0:T(8,128)}), f32[32,1024]{1,0:T(8,128)}) %reduce-scatter.21.cloned.1.call-update) | async-done | bytes 131088 | tf_op jit(solution)/shard_map/reduce_scatter | solution.py:269
  495.9 74.6 %reduce-scatter.19.cloned.1.call-done = f32[256,32]{0,1:T(8,128)} async-done(((f32[256,512]{0,1:T(8,128)}), f32[256,32]{0,1:T(8,128)}) %reduce-scatter.19.cloned.1.call-update) | async-done | bytes 32784 | tf_op jit(solution)/shard_map/reduce_scatter | solution.py:268
  571.9 76.3 %reduce-scatter.17.cloned.1.call-done = f32[32,3,256]{2,0,1:T(8,128)} async-done(((f32[512,3,256]{2,0,1:T(8,128)}), f32[32,3,256]{2,0,1:T(8,128)}) %reduce-scatter.17.cloned.1.call-update) | async-done | bytes 98320 | tf_op jit(solution)/shard_map/reduce_scatter | solution.py:267
  649.8 6.8 reduce-scatter.15.cloned.1.call-done
  659.3 40.7 %all-reduce = (f32[512]{0:T(512)S(1)}, f32[512]{0:T(512)S(1)}, f32[512]{0:T(512)S(1)}, f32[2048]{0:T(1024)S(1)}, f32[512]{0:T(512)S(1)}) all-reduce(f32[512]{0:T(512)S(1)} %get-tuple-element.489, f32[512]{0:T(512)S(1)} %get-tuple-element.564, f32[512]{0:T(512)S(1)} %get-tuple-element.487, ...), channel_id=1, replica_groups=mesh['dp'=16,'tensor'=2] {'dp','tensor'}, use_global_device_ids=true, to_apply=%region_26.27 | all-reduce | flops 4096 | bytes 32768 | tf_op jit(solution)/shard_map/psum | solution.py:256
  702.9 2.9 fusion.140
  (250 shorter events, 104.9 us)
Async XLA Ops:
  8.0 3.3 copy-start
  8.0 3.3 copy-start.16
  8.0 89.3 %all-gather.8.cloned.1.call-start = ((), (), s32[]{:S(2)}) async-start(), calls=%async_computation.8 | async-start | bytes 3145728 | tf_op jit(solution)/shard_map/all_gather | solution.py:36
  9.6 3.3 copy-start.12
  9.6 3.4 copy-start.14
  12.8 47.6 %copy-start.18 = (bf16[256,32]{0,1:T(8,128)(2,1)S(1)}, bf16[256,32]{0,1:T(8,128)(2,1)}, u32[]{:S(2)}) copy-start(bf16[256,32]{0,1:T(8,128)(2,1)} %param.23) | copy-start | bytes 49156
  12.8 130.9 %reduce-scatter.9.cloned.1.call-start = ((), (), s32[]{:S(2)}) async-start(), calls=%async_computation.9 | async-start | bytes 3145728 | tf_op jit(solution)/shard_map/reduce_scatter | solution.py:40
  60.4 42.1 %copy-start.10 = (bf16[512,3,256]{0,2,1:T(8,128)(2,1)}, bf16[512,3,256]{0,2,1:T(8,128)(2,1)S(1)}, u32[]{:S(2)}) copy-start(bf16[512,3,256]{0,2,1:T(8,128)(2,1)S(1)} %copy.63) | copy-start | bytes 2359300
  130.4 2.5 copy-start.23
  133.9 9.7 %copy-start.13 = (f32[512]{0:T(512)S(1)}, f32[512]{0:T(512)}, u32[]{:S(2)}) copy-start(f32[512]{0:T(512)} %param.24) | copy-start | bytes 6148
  136.1 56.8 %all-gather.12.cloned.1.call-start = ((), (), s32[]{:S(2)}) async-start(), calls=%async_computation.11 | async-start | bytes 1114112 | tf_op jit(solution)/shard_map/all_gather | solution.py:132
  136.7 9.4 %copy-start.17 = (f32[512]{0:T(512)S(1)}, f32[512]{0:T(512)}, u32[]{:S(2)}) copy-start(f32[512]{0:T(512)} %param.25) | copy-start | bytes 6148
  136.7 67.6 %all-gather.10.cloned.1.call-start = ((), (), s32[]{:S(2)}) async-start(), calls=%async_computation.10 | async-start | bytes 3145728 | tf_op jit(solution)/shard_map/all_gather | solution.py:36
  146.1 58.3 %copy-start.22 = (f32[1024]{0:T(1024)S(1)}, f32[1024]{0:T(1024)}, u32[]{:S(2)}) copy-start(f32[1024]{0:T(1024)} %param.27) | copy-start | bytes 12292
  147.6 116.3 %all-gather.14.cloned.1.call-start = ((), (), s32[]{:S(2)}) async-start(), calls=%async_computation.12 | async-start | bytes 1114112 | tf_op jit(solution)/shard_map/all_gather | solution.py:133
  148.2 126.7 %all-gather.18.cloned.1.call-start = ((), (), s32[]{:S(2)}) async-start(), calls=%async_computation.21 | async-start | bytes 3145728 | tf_op jit(solution)/shard_map/all_gather | solution.py:36
  148.9 152.9 %reduce-scatter.13.cloned.1.call-start = ((), (), s32[]{:S(2)}) async-start(), calls=%async_computation.14 | async-start | bytes 3145728 | tf_op jit(solution)/shard_map/reduce_scatter | solution.py:40
  274.9 12.1 %copy-start.21 = (bf16[512,1024]{1,0:T(8,128)(2,1)S(1)}, bf16[512,1024]{1,0:T(8,128)(2,1)}, u32[]{:S(2)}) copy-start(bf16[512,1024]{1,0:T(8,128)(2,1)} %all-gather.12.cloned.1.call-done) | copy-start | bytes 3145732
  290.9 23.9 %reduce-scatter.11.cloned.1.call-start = ((), (), s32[]{:S(2)}) async-start(), calls=%async_computation.13 | async-start | bytes 3145728 | tf_op jit(solution)/shard_map/reduce_scatter | solution.py:40
  297.5 17.2 %copy-start.19 = (f32[512]{0:T(512)S(1)}, f32[512]{0:T(512)}, u32[]{:S(2)}) copy-start(f32[512]{0:T(512)} %param.29) | copy-start | bytes 6148
  297.5 35.6 %all-gather.16.cloned.1.call-start = ((), (), s32[]{:S(2)}) async-start(), calls=%async_computation.15 | async-start | bytes 3145728 | tf_op jit(solution)/shard_map/all_gather | solution.py:36
  318.9 96.1 %reduce-scatter.23.cloned.1.call-start = ((), (), s32[]{:S(2)}) async-start(), calls=%async_computation.20 | async-start | bytes 2228224 | tf_op jit(solution)/shard_map/reduce_scatter | solution.py:270
  325.6 168.7 %reduce-scatter.21.cloned.1.call-start = ((), (), s32[]{:S(2)}) async-start(), calls=%async_computation.19 | async-start | bytes 2228224 | tf_op jit(solution)/shard_map/reduce_scatter | solution.py:269
  332.9 237.6 %reduce-scatter.19.cloned.1.call-start = ((), (), s32[]{:S(2)}) async-start(), calls=%async_computation.18 | async-start | bytes 557056 | tf_op jit(solution)/shard_map/reduce_scatter | solution.py:268
  336.4 4.9 copy-start.3
  336.4 4.9 copy-start.15
  336.4 4.9 copy-start.24
  377.6 270.6 %reduce-scatter.17.cloned.1.call-start = ((), (), s32[]{:S(2)}) async-start(), calls=%async_computation.17 | async-start | bytes 1671168 | tf_op jit(solution)/shard_map/reduce_scatter | solution.py:267
  384.6 2.8 copy-start.20
  387.4 3.3 copy-start.11
  390.5 266.1 %reduce-scatter.15.cloned.1.call-start = ((), (), s32[]{:S(2)}) async-start(), calls=%async_computation.16 | async-start | bytes 3145728 | tf_op jit(solution)/shard_map/reduce_scatter | solution.py:40
  656.6 46.3 %copy-start.6 = (bf16[1024,512]{1,0:T(8,128)(2,1)S(1)}, bf16[1024,512]{1,0:T(8,128)(2,1)}, u32[]{:S(2)}) copy-start(bf16[1024,512]{1,0:T(8,128)(2,1)} %reduce-scatter.15.cloned.1.call-done) | copy-start | bytes 3145732
  (8 other events, 13.4 us)
Sparse Core Ops, SparseCore 0:
  12.9 13.2 all-gather.7
  136.2 7.3 reduce-scatter.8
  291.0 10.8 reduce-scatter.12
  303.9 10.7 reduce-scatter.10
Sparse Core Ops, SparseCore 1:
  139.7 53.1 all-gather.11
  195.0 9.3 all-gather.9
  207.3 56.5 all-gather.13
  265.6 9.3 all-gather.17
  319.0 11.6 all-gather.15
  333.1 81.9 reduce-scatter.22
  417.3 77.0 reduce-scatter.20
  497.1 73.4 reduce-scatter.18
  572.7 75.5 reduce-scatter.16
  650.6 6.0 reduce-scatter.14
where the time goes:
time: 723 us; the launch traced here: 713 us
  waiting for transfers between devices  391 us (54%)
  blocking collectives  125 us (17%)
  matrix products  112 us (15%)
  other arithmetic  34.3 us (5%)
  local copies, waits for them, and re-layouts  32.8 us (5%)
  between operations  16 us (2%)
    reduce_scatter x1, waiting for transfers between devices, shards(): lax.psum_scatter(grad_up, 'dp', scatter_dimension=0, tiled=True)  77.7 us
    reduce_scatter x1, waiting for transfers between devices, shards(): lax.psum_scatter(grad_qkv, 'dp', scatter_dimension=0, tiled=True)  76.3 us
    reduce_scatter x1, waiting for transfers between devices, shards(): lax.psum_scatter(grad_wout, 'dp', scatter_dimension=1, tiled=True)  74.6 us
    all_gather x1, waiting for transfers between devices, shards(): lax.all_gather(w_down, 'dp', axis=1, tiled=True)  49.1 us
    all_gather x1, blocking collectives, shards(): lax.all_gather(w_qkv, 'dp', axis=0, tiled=True)  47 us
    all_gather x1, waiting for transfers between devices, shards(): lax.all_gather(w_up, 'dp', axis=0, tiled=True)  43.8 us
    psum x1, blocking collectives, shards(): lax.psum((gain_one_part, gain_two_part, jnp.sum(grad_branch, axis=0, dtyp...  40.7 us
    all_gather x1, blocking collectives, shards(): lax.all_gather(w_out, 'dp', axis=1, tiled=True)  36.9 us
  transfers between devices with their start and end apart: 14, of which 12 were waited for; matrix products, arithmetic and copies ran while one was open for 15% of the time, Pallas kernels for 0%

commit v1 on v0

v1 whole, which is shorter than its diff:
```python
import functools
import math

import jax
import jax.numpy as jnp
from jax import lax
from jax.experimental import pallas as pl
from jax.experimental.pallas import tpu as pltpu
from jax.sharding import PartitionSpec as P

HD = 64
BLK = 256
EPS = 1e-05
MASKED = -1e30
Z = 4
YX = 4
GROUPS = Z * YX
F32 = jnp.float32
BF = jnp.bfloat16
MESH = pl.DeviceIdType.MESH


def dot(a, b, ca, cb):
    return lax.dot_general(a, b, (((ca,), (cb,)), ((), ())), preferred_element_type=F32)


def nn(a, b):
    return dot(a, b, 1, 0)


def nt(a, b):
    return dot(a, b, 1, 1)


def tn(a, b):
    return dot(a, b, 0, 0)


def iota(shape, axis):
    return lax.broadcasted_iota(jnp.int32, shape, axis)


def unit_rows(values):
    centre = values - jnp.mean(values, axis=-1, keepdims=True)
    spread = jnp.mean(centre * centre, axis=-1, keepdims=True)
    inverse = lax.rsqrt(spread + EPS)
    return centre * inverse, inverse


def eight(values):
    return jnp.sum(values.reshape(values.shape[0] // 8, 8, values.shape[1]), axis=0)


class Sizes:
    pass


def kernel(s, *refs):
    (tok, cot, span, gain1, gain2, bout, bdown, bup_own, shard) = refs[:9]
    (res, dtok, gpack, o_gain1, o_gain2, o_bout, o_bdown, o_bup) = refs[9:17]
    (W, G, R0, R1, R2, R3, H1, H1T, QKV, PT, PF, O, MID, H2, H2T, COTT, HID, GI, GB, GBT,
     BUP, KSV, KB, VB, DKS, DVS, DSV, DSVR, SHARE, SPC, M8, BUACC, ACC, SM, SMR,
     ag_s, ag_r, rs_s, rs_r, sx_s, sx_r) = refs[17:]
    D, H2W, F2, rows_n, NB = s.D, s.H2W, s.F2, s.rows, s.NB
    QW = 3 * H2W
    C_OUT, C_UP, C_DN = QW, QW + H2W, QW + H2W + F2
    d = lax.axis_index("dp")
    t = lax.axis_index("tensor")
    g = d // s.sub
    z = g // YX
    yx = g % YX
    rest = d % s.sub
    b2 = 2 - t
    b3 = 1 + t

    def at(zz, q):
        return ((zz * YX + q) * s.sub + rest, t)

    def flip(q, bit):
        y_bit, x_bit = q // 2, q % 2
        return jnp.where(bit == 2, (1 - y_bit) * 2 + x_bit, y_bit * 2 + 1 - x_bit)

    yx2 = flip(yx, b2)
    yx3 = flip(yx, b3)
    yx23 = 3 - yx
    pair = (d, 1 - t)
    peer2 = at(z, yx2)
    peer3 = at(z, yx3)
    zpeers = [at((z + k) % Z, yx) for k in range(1, Z)]

    barrier = pltpu.get_barrier_semaphore()
    for who in [pair, peer2, peer3] + zpeers:
        pl.semaphore_signal(barrier, inc=1, device_id=who, device_id_type=MESH)

    W[t, z, yx] = shard[...]
    BUP[t] = jnp.broadcast_to(bup_own[...], (8, F2))

    pl.semaphore_wait(barrier, 3 + Z - 1)

    def remote(src, dst, ss, rs, who):
        return pltpu.make_async_remote_copy(
            src_ref=src, dst_ref=dst, send_sem=ss, recv_sem=rs, device_id=who, device_id_type=MESH
        )

    chunks = s.ag_chunks

    def ag_copy(c, kind):
        lo, n = chunks[c]
        cols = pl.ds(lo, n)
        if kind < 3:
            window, who = W.at[t, z, yx, :, cols], zpeers[kind]
        else:
            group, who = {
                3: (yx, peer2),
                4: (yx, peer3),
                5: (yx2, peer3),
                6: (yx, pair),
                7: (yx2, pair),
                8: (yx3, pair),
                9: (yx23, pair),
            }[kind]
            window = W.at[t, :, group, :, cols]
        return remote(window, window, ag_s.at[c, kind], ag_r.at[c, kind], who)

    def ag_recv(c, kind):
        lo, n = chunks[c]
        cols = pl.ds(lo, n)
        if kind < 3:
            window = W.at[t, (z + Z - 1 - kind) % Z, yx, :, cols]
        elif kind < 6:
            window = W.at[t, :, {3: yx2, 4: yx3, 5: yx23}[kind], :, cols]
        else:
            window = W.at[1 - t, :, {6: yx, 7: yx2, 8: yx3, 9: yx23}[kind], :, cols]
        remote(window, window, ag_s.at[c, kind], ag_r.at[c, kind], pair).wait_recv()

    def ag_start(c, kinds):
        for kind in kinds:
            ag_copy(c, kind).start()

    def ag0(c):
        ag_start(c, (0, 1, 2))

    def ag1(c):
        for kind in (0, 1, 2):
            ag_recv(c, kind)
        ag_start(c, (3, 4, 6))

    def ag2(c):
        ag_recv(c, 3)
        ag_start(c, (5, 7))

    def ag3(c):
        ag_recv(c, 4)
        ag_start(c, (8,))
        ag_recv(c, 5)
        ag_start(c, (9,))

    def ag4(c):
        for kind in (6, 7, 8, 9):
            ag_recv(c, kind)

    def small_copy(i, src, dst, who):
        return remote(src, dst, sx_s.at[i], sx_r.at[i], who)

    for c in range(len(chunks)):
        ag0(c)
    bup_copy = small_copy(0, BUP.at[t], BUP.at[t], pair)
    bup_copy.start()

    def wl(half, lo, n):
        return W[half, :, :, :, pl.ds(lo, n)].reshape(D, n)

    def rows_of(b):
        return pl.ds(pl.multiple_of(b * BLK, BLK), BLK)

    def norm_one(b, _):
        r = rows_of(b)
        unit, _inv = unit_rows(tok[r, :].astype(F32))
        low = (unit * gain1[...]).astype(BF)
        H1[r, :] = low
        H1T[:, r] = low.T
        COTT[:, r] = cot[r, :].T
        return 0

    lax.fori_loop(0, NB, norm_one, 0)

    half_rows = iota((8, BLK), 0)
    for b in range(NB):
        line = span[pl.ds(t * NB + b, 1), :]
        belongs = jnp.logical_and(half_rows // NB == line, half_rows % NB == b)
        M8[:, b * BLK:(b + 1) * BLK] = belongs.astype(F32)
    SPC[...] = jnp.concatenate([span[...].astype(F32), jnp.zeros((120, BLK), F32)], axis=0).T
    zeros_in = (span[...] == 0).astype(F32)
    ones_in = (span[...] == 1).astype(F32)
    n_zero = jnp.sum(zeros_in, axis=1, keepdims=True)
    n_one = jnp.sum(ones_in, axis=1, keepdims=True)
    counts = jnp.concatenate(
        [n_zero[:NB], n_one[:NB], n_zero[NB:2 * NB], n_one[NB:2 * NB]], axis=0
    )
    log_counts = jnp.concatenate([jnp.log(counts)] * 4, axis=0)
    own_counts = jnp.sum(M8[...], axis=1, keepdims=True)
    code = iota((64, 1), 0) % 16
    block_of = (code // 8) * NB + code % NB

    BUACC[...] = jnp.zeros_like(BUACC)
    ACC[...] = jnp.zeros_like(ACC)
    DKS[...] = jnp.zeros_like(DKS)
    DVS[...] = jnp.zeros_like(DVS)

    ag1(0)
    ag2(0)
    ag1(1)
    ag3(0)
    ag4(0)

    q_scale = jnp.where(iota((1, QW), 1) < H2W, 1.0 / math.sqrt(HD), 1.0).astype(F32)

    def project(i, _):
        b, half = i // 2, i % 2
        r = rows_of(b)
        y = nn(H1[r, :], wl(half, 0, QW)) * q_scale
        QKV[half, r, :] = y.astype(BF)
        return 0

    lax.fori_loop(0, 2 * NB, project, 0)
    ag2(1)

    member_low = jnp.concatenate([M8[...], M8[...]], axis=0).astype(BF)
    for half in range(2):
        sums = nn(member_low, QKV[half, :, H2W:])[:8]
        means = (sums / own_counts).astype(BF).astype(F32)
        KSV[t, :, pl.ds(half * 2 * H2W, 2 * H2W)] = means
    ksv_copy = small_copy(1, KSV.at[t], KSV.at[t], pair)
    ksv_copy.start()
    ag3(1)
    small_copy(1, KSV.at[1 - t], KSV.at[1 - t], pair).wait_recv()
    diagonal = iota((64, H2W), 0) // 16 == iota((64, H2W), 1) // HD
    everything = KSV[...].reshape(16, 4 * H2W)
    for half in range(2):
        for kind, out in ((0, KB), (1, VB)):
            lo = (2 * half + kind) * H2W
            tiled = jnp.concatenate([everything[:, lo:lo + H2W]] * 4, axis=0)
            out[half] = jnp.where(diagonal, tiled, 0.0).astype(BF)

    even = iota((BLK, 128), 1) < HD

    def head_only(values, e):
        return jnp.where(even if e == 0 else jnp.logical_not(even), values, jnp.zeros_like(values))

    def attend(i, _):
        b, half = i // 2, i % 2
        r = rows_of(b)
        q = QKV[half, r, 0:H2W]
        far = nt(KB[half], q) + log_counts
        far = jnp.where(block_of < t * NB + b, far, MASKED)
        parts, far_parts = [], []
        for pr in range(2):
            lanes = slice(pr * 128, (pr + 1) * 128)
            q2 = q[:, lanes]
            k2 = QKV[half, r, H2W + pr * 128:H2W + (pr + 1) * 128]
            v2 = QKV[half, r, 2 * H2W + pr * 128:2 * H2W + (pr + 1) * 128]
            both = []
            for e in range(2):
                hl = 2 * pr + e
                near = nt(k2, head_only(q2, e))
                sf = far[16 * hl:16 * hl + 16]
                largest = jnp.maximum(
                    jnp.max(near, axis=0, keepdims=True), jnp.max(sf, axis=0, keepdims=True)
                )
                pn = jnp.exp(near - largest)
                pf = jnp.exp(sf - largest)
                total = jnp.sum(pn, axis=0, keepdims=True) + jnp.sum(pf, axis=0, keepdims=True)
                inv = 1.0 / total
                pn = (pn * inv).astype(BF)
                PT[half, b, hl] = pn
                far_parts.append(pf * inv)
                both.append(tn(pn, v2))
            parts.append(jnp.where(even, both[0], both[1]))
        pf_all = jnp.concatenate(far_parts, axis=0).astype(BF)
        PF[half, b] = pf_all
        out = jnp.concatenate(parts, axis=1) + tn(pf_all, VB[half])
        O[half, r, :] = out.astype(BF)
        for when, todo in s.fwd_slots:
            @pl.when(i == when)
            def _():
                for name, c in todo:
                    {"1": ag1, "2": ag2, "3": ag3, "4": ag4}[name](c)
        return 0

    lax.fori_loop(0, 2 * NB, attend, 0)

    small_copy(0, BUP.at[1 - t], BUP.at[1 - t], pair).wait_recv()

    def out_proj(b, _):
        r = rows_of(b)
        branch = nt(O[0, r, :], wl(0, C_OUT, H2W)) + nt(O[1, r, :], wl(1, C_OUT, H2W))
        middle = tok[r, :].astype(F32) + (branch + bout[...])
        MID[r, :] = middle
        unit, _inv = unit_rows(middle)
        low = (unit * gain2[...]).astype(BF)
        H2[r, :] = low
        H2T[:, r] = low.T
        return 0

    lax.fori_loop(0, NB, out_proj, 0)

    for name, c in s.tail_slots:
        {"1": ag1, "2": ag2, "3": ag3, "4": ag4}[name](c)

    FC = 512
    NFC = F2 // FC
    c0 = math.sqrt(2.0 / math.pi)
    c1 = c0 * 0.044715

    def feed(i, _):
        b = i // (2 * NFC)
        half = (i // NFC) % 2
        fc = pl.multiple_of((i % NFC) * FC, FC)
        r = rows_of(b)
        x = nn(H2[r, :], wl(half, pl.multiple_of(C_UP + fc, FC), FC)) + BUP[half, 0:1, pl.ds(fc, FC)]
        gh = nn(cot[r, :], wl(half, pl.multiple_of(C_DN + fc, FC), FC))
        sq = x * x
        th = jnp.tanh(x * (c0 + c1 * sq))
        up = 0.5 + 0.5 * th
        HID[half, r, pl.ds(fc, FC)] = (x * up).astype(BF)
        slope = up + (0.5 * x) * (1.0 - th * th) * (c0 + (3.0 * c1) * sq)
        gi = gh * slope
        GI[half, r, pl.ds(fc, FC)] = gi.astype(BF)
        BUACC[half, :, pl.ds(fc, FC)] += eight(gi)
        return 0

    lax.fori_loop(0, 2 * NB * NFC, feed, 0)

    def feed_back(b, _):
        r = rows_of(b)
        down = nt(HID[0, r, :], wl(0, C_DN, F2)) + nt(HID[1, r, :], wl(1, C_DN, F2))
        middle = MID[r, :]
        res[r, :] = (middle + (down + bdown[...])).astype(BF)
        g2 = nt(GI[0, r, :], wl(0, C_UP, F2)) + nt(GI[1, r, :], wl(1, C_UP, F2))
        unit, inverse = unit_rows(middle)
        e = g2 * gain2[...]
        m1 = jnp.mean(e, axis=-1, keepdims=True)
        m2 = jnp.mean(e * unit, axis=-1, keepdims=True)
        grad_out = cot[r, :].astype(F32)
        mid = grad_out + inverse * (e - m1 - unit * m2)
        MID[r, :] = mid
        low = mid.astype(BF)
        GB[r, :] = low
        GBT[:, r] = low.T
        ACC[1] += eight(g2 * unit)
        ACC[2] += eight(mid)
        ACC[3] += eight(grad_out)
        return 0

    lax.fori_loop(0, NB, feed_back, 0)

    rchunks = s.rs_chunks

    def rs_copy(c, kind):
        lo, n = rchunks[c]
        cols = pl.ds(lo, n)
        if kind == 0:
            src, dst, who = G.at[1 - t, :, :, :, cols], R0.at[:, :, :, cols], pair
        elif kind == 1:
            src, dst, who = G.at[t, :, yx3, :, cols], R1.at[0, :, :, cols], peer3
        elif kind == 2:
            src, dst, who = G.at[t, :, yx23, :, cols], R1.at[1, :, :, cols], peer3
        elif kind == 3:
            src, dst, who = G.at[t, :, yx2, :, cols], R2.at[:, :, cols], peer2
        else:
            k = kind - 3
            src, dst, who = G.at[t, (z + k) % Z, yx, :, cols], R3.at[k - 1, :, cols], zpeers[k - 1]
        return remote(src, dst, rs_s.at[c, kind], rs_r.at[c, kind], who)

    def rs0(c):
        rs_copy(c, 0).start()

    def rs1(c):
        lo, n = rchunks[c]
        rs_copy(c, 0).wait_recv()
        cols = pl.ds(lo, n)

        def add(q):
            for zz in range(Z):
                G[t, zz, q, :, cols] = (
                    G[t, zz, q, :, cols].astype(F32) + R0[zz, q, :, cols].astype(F32)
                ).astype(BF)

        add(yx23)
        rs_copy(c, 2).start()
        add(yx3)
        rs_copy(c, 1).start()
        add(yx2)
        add(yx)

    def rs2(c):
        lo, n = rchunks[c]
        cols = pl.ds(lo, n)

        def add(q, j):
            for zz in range(Z):
                G[t, zz, q, :, cols] = (
                    G[t, zz, q, :, cols].astype(F32) + R1[j, zz, :, cols].astype(F32)
                ).astype(BF)

        rs_copy(c, 2).wait_recv()
        add(yx2, 1)
        rs_copy(c, 3).start()
        rs_copy(c, 1).wait_recv()
        add(yx, 0)

    def rs3(c):
        lo, n = rchunks[c]
        cols = pl.ds(lo, n)
        rs_copy(c, 3).wait_recv()
        for zz in range(Z):
            G[t, zz, yx, :, cols] = (
                G[t, zz, yx, :, cols].astype(F32) + R2[zz, :, cols].astype(F32)
            ).astype(BF)
        for kind in (4, 5, 6):
            rs_copy(c, kind).start()

    def rs4(c):
        lo, n = rchunks[c]
        cols = pl.ds(lo, n)
        total = G[t, z, yx, :, cols].astype(F32)
        for kind in (4, 5, 6):
            rs_copy(c, kind).wait_recv()
            total = total + R3[kind - 4, :, cols].astype(F32)
        gpack[:, cols] = total * s.factor

    rs_steps = {"0": rs0, "1": rs1, "2": rs2, "3": rs3, "4": rs4}

    def weight_grad(lhs, rhs, c_lo, width, step):
        per = width // step

        def one(i, _):
            half = i // per
            lo = pl.multiple_of((i % per) * step, 128)
            y = nn(lhs[...], rhs[half, :, pl.ds(lo, step)]).astype(BF)
            G[half, :, :, :, pl.ds(pl.multiple_of(c_lo + lo, 128), step)] = y.reshape(Z, YX, D // GROUPS, step)
            return 0

        lax.fori_loop(0, 2 * per, one, 0)

    weight_grad(COTT, HID, C_DN, F2, 512)
    rs0(0)
    weight_grad(H2T, GI, C_UP, F2, 512)
    rs0(1)
    rs1(0)

    GP = HID

    weight_grad(GBT, O, C_OUT, H2W, H2W)
    rs0(2)
    rs1(1)

    def attend_back(i, _):
        b, half = i // 2, i % 2
        r = rows_of(b)
        do = nn(GB[r, :], wl(half, C_OUT, H2W)).astype(BF)
        q = QKV[half, r, 0:H2W]
        dpf = nt(VB[half], do)
        pf_low = PF[half, b]
        pf_all = pf_low.astype(F32)
        far_parts = []
        for pr in range(2):
            lanes = slice(pr * 128, (pr + 1) * 128)
            q2 = q[:, lanes]
            do2 = do[:, lanes]
            k2 = QKV[half, r, H2W + pr * 128:H2W + (pr + 1) * 128]
            v2 = QKV[half, r, 2 * H2W + pr * 128:2 * H2W + (pr + 1) * 128]
            dqs, dks, dvs = [], [], []
            for e in range(2):
                hl = 2 * pr + e
                dp = nt(v2, head_only(do2, e))
                p_low = PT[half, b, hl]
                p = p_low.astype(F32)
                df = dpf[16 * hl:16 * hl + 16]
                pf = pf_all[16 * hl:16 * hl + 16]
                corr = jnp.sum(p * dp, axis=0, keepdims=True) + jnp.sum(pf * df, axis=0, keepdims=True)
                ds = (p * (dp - corr)).astype(BF)
                far_parts.append(pf * (df - corr))
                dqs.append(tn(ds, k2))
                dks.append(nn(ds, q2))
                dvs.append(nn(p_low, do2))
            GP[half, r, H2W + pr * 128:H2W + (pr + 1) * 128] = jnp.where(even, dks[0], dks[1]).astype(BF)
            GP[half, r, 2 * H2W + pr * 128:2 * H2W + (pr + 1) * 128] = jnp.where(even, dvs[0], dvs[1]).astype(BF)
            MQ = jnp.where(even, dqs[0], dqs[1])
            if pr == 0:
                dq0 = MQ
            else:
                dq = jnp.concatenate([dq0, MQ], axis=1)
        dsf = jnp.concatenate(far_parts, axis=0).astype(BF)
        dq = (dq + tn(dsf, KB[half])) * (1.0 / math.sqrt(HD))
        GP[half, r, 0:H2W] = dq.astype(BF)
        DKS[half] += nn(dsf, q)
        DVS[half] += nn(pf_low, do)
        for when, todo in s.bwd_slots:
            @pl.when(i == when)
            def _():
                for name, c in todo:
                    rs_steps[name](c)
        return 0

    lax.fori_loop(0, 2 * NB, attend_back, 0)

    for half in range(2):
        for kind, src in ((0, DKS), (1, DVS)):
            kept = jnp.where(diagonal, src[half], 0.0)
            folded = kept[0:16] + kept[16:32] + kept[32:48] + kept[48:64]
            lo = (2 * half + kind) * H2W
            DSV[:, :, lo:lo + H2W] = folded.reshape(2, 8, H2W)
    dsv_copy = small_copy(2, DSV.at[1 - t], DSVR, pair)
    dsv_copy.start()
    dsv_copy.wait_recv()
    SHARE[...] = (DSV[t] + DSVR[...]) / own_counts

    for name, c in s.mid_slots:
        rs_steps[name](c)

    span_lane = iota((BLK, 128), 1)

    def last(b, _):
        r = rows_of(b)
        column = jnp.sum(jnp.where(span_lane == t * NB + b, SPC[...], 0.0), axis=1, keepdims=True)
        grad = None
        for half in range(2):
            lanes = slice(half * 2 * H2W, (half + 1) * 2 * H2W)
            shared = jnp.where(column == 0.0, SHARE[pl.ds(b, 1), lanes], SHARE[pl.ds(NB + b, 1), lanes])
            GP[half, r, H2W:QW] = (GP[half, r, H2W:QW].astype(F32) + shared).astype(BF)
            part = nt(GP[half, r, 0:QW], wl(half, 0, QW))
            grad = part if grad is None else grad + part
        unit, inverse = unit_rows(tok[r, :].astype(F32))
        e = grad * gain1[...]
        m1 = jnp.mean(e, axis=-1, keepdims=True)
        m2 = jnp.mean(e * unit, axis=-1, keepdims=True)
        dtok[r, :] = (MID[r, :] + inverse * (e - m1 - unit * m2)).astype(BF)
        ACC[0] += eight(grad * unit)
        return 0

    lax.fori_loop(0, NB, last, 0)

    weight_grad(H1T, GP, 0, QW, 384)
    rs0(3)

    folded = [jnp.sum(ACC[j], axis=0, keepdims=True) for j in range(4)]
    for half in range(2):
        line = jnp.sum(BUACC[half], axis=0, keepdims=True)
        folded += [line[:, j * D:(j + 1) * D] for j in range(F2 // D)]
    SM[0] = jnp.concatenate(folded, axis=0)

    def exchange(i, who):
        cp = small_copy(3 + i, SM.at[i], SMR.at[i], who)
        cp.start()
        cp.wait_recv()
        return SM[i] + SMR[i]

    SM[1] = exchange(0, pair)
    rs1(3)
    SM[2] = exchange(1, peer3)
    rs2(3)
    total = exchange(2, peer2)
    rs3(3)
    SM[3] = total
    for k in range(1, Z):
        small_copy(5 + k, SM.at[3], SMR.at[3 + (z + 0) % Z], zpeers[k - 1]).start()
    SMR[3 + z] = total
    for k in range(1, Z):
        small_copy(5 + k, SM.at[3], SMR.at[3 + (z + Z - k) % Z], zpeers[k - 1]).wait_recv()
    summed = (SMR[3] + SMR[4] + SMR[5] + SMR[6]) * s.factor
    o_gain1[...] = summed[0:1]
    o_gain2[...] = summed[1:2]
    o_bout[...] = summed[2:3]
    o_bdown[...] = summed[3:4]
    for j in range(2 * F2 // D):
        o_bup[:, j * D:(j + 1) * D] = summed[4 + j:5 + j]

    for name, c in s.end_slots:
        rs_steps[name](c)

    for c in range(len(chunks)):
        for kind in range(10):
            ag_copy(c, kind).wait_send()
    for c in range(len(rchunks)):
        for kind in range(7):
            rs_copy(c, kind).wait_send()
    bup_copy.wait_send()
    ksv_copy.wait_send()
    dsv_copy.wait_send()
    for i, who in enumerate((pair, peer3, peer2)):
        small_copy(3 + i, SM.at[i], SMR.at[i], who).wait_send()
    for k in range(1, Z):
        small_copy(5 + k, SM.at[3], SMR.at[3 + z], zpeers[k - 1]).wait_send()


def shards(
    tokens, cotangent, span_ids, gain_one, w_qkv, w_out, b_out, gain_two, w_up, b_up, w_down, b_down
):
    s = Sizes()
    dp = lax.axis_size("dp")
    s.sub = dp // GROUPS
    s.D = tokens.shape[2]
    s.rows = tokens.shape[1]
    s.NB = s.rows // BLK
    s.H2W = w_qkv.shape[2]
    s.F2 = w_up.shape[1]
    s.factor = 1.0 / math.sqrt(dp * lax.axis_size("tensor") * s.rows)
    sub, D, H2W, F2, N, NB = s.sub, s.D, s.H2W, s.F2, s.rows, s.NB
    QW = 3 * H2W
    width = QW + H2W + 2 * F2
    s.ag_chunks = [(0, 768), (768, 768), (1536, 768), (2304, 768)]
    s.rs_chunks = [(QW + H2W + F2, F2), (QW + H2W, F2), (QW, H2W), (0, QW)]
    s.fwd_slots = [(0, [("1", 2)]), (1, [("2", 2)]), (2, [("4", 1)]), (3, [("1", 3)]), (4, [("3", 2)]), (5, [("2", 3)])]
    s.tail_slots = [("4", 2), ("3", 3), ("4", 3)]
    s.bwd_slots = [(0, [("2", 0)]), (1, [("1", 2)]), (2, [("2", 1)]), (3, [("3", 0)]), (4, [("2", 2)]), (5, [("3", 1)]), (6, [("4", 0)]), (7, [("3", 2)])]
    s.mid_slots = [("4", 1), ("4", 2)]
    s.end_slots = [("4", 3)]
    pack = jnp.concatenate(
        [w_qkv.reshape(w_qkv.shape[0], QW), w_out.T, w_up, w_down.T], axis=1
    )
    groups = [[a * sub + b for b in range(sub)] for a in range(dp // sub)]
    if sub > 1:
        pack = lax.all_gather(pack, "dp", axis=0, tiled=True, axis_index_groups=groups)
    R = D // GROUPS

    def vm(*shape, dtype=BF):
        return pltpu.VMEM(shape, dtype)

    out = pl.pallas_call(
        functools.partial(kernel, s),
        out_shape=(
            jax.ShapeDtypeStruct((N, D), BF),
            jax.ShapeDtypeStruct((N, D), BF),
            jax.ShapeDtypeStruct((R, width), F32),
            jax.ShapeDtypeStruct((1, D), F32),
            jax.ShapeDtypeStruct((1, D), F32),
            jax.ShapeDtypeStruct((1, D), F32),
            jax.ShapeDtypeStruct((1, D), F32),
            jax.ShapeDtypeStruct((1, 2 * F2), F32),
        ),
        in_specs=[pl.BlockSpec(memory_space=pltpu.VMEM)] * 9,
        out_specs=[pl.BlockSpec(memory_space=pltpu.VMEM)] * 8,
        scratch_shapes=[
            vm(2, Z, YX, R, width),
            vm(2, Z, YX, R, width),
            vm(Z, YX, R, width),
            vm(2, Z, R, width),
            vm(Z, R, width),
            vm(Z - 1, R, width),
            vm(N, D),
            vm(D, N),
            vm(2, N, QW),
            vm(2, NB, 4, BLK, BLK),
            vm(2, NB, 64, BLK),
            vm(2, N, H2W),
            vm(N, D, dtype=F32),
            vm(N, D),
            vm(D, N),
            vm(D, N),
            vm(2, N, F2),
            vm(2, N, F2),
            vm(N, D),
            vm(D, N),
            vm(2, 8, F2, dtype=F32),
            vm(2, 8, 4 * H2W, dtype=F32),
            vm(2, 64, H2W),
            vm(2, 64, H2W),
            vm(2, 64, H2W, dtype=F32),
            vm(2, 64, H2W, dtype=F32),
            vm(2, 8, 4 * H2W, dtype=F32),
            vm(8, 4 * H2W, dtype=F32),
            vm(8, 4 * H2W, dtype=F32),
            vm(BLK, 128, dtype=F32),
            vm(8, N, dtype=F32),
            vm(2, 8, F2, dtype=F32),
            vm(4, 8, D, dtype=F32),
            vm(4, 8, D, dtype=F32),
            vm(7, 8, D, dtype=F32),
            pltpu.SemaphoreType.DMA((len(s.ag_chunks), 10)),
            pltpu.SemaphoreType.DMA((len(s.ag_chunks), 10)),
            pltpu.SemaphoreType.DMA((len(s.rs_chunks), 7)),
            pltpu.SemaphoreType.DMA((len(s.rs_chunks), 7)),
            pltpu.SemaphoreType.DMA((9,)),
            pltpu.SemaphoreType.DMA((9,)),
        ],
        compiler_params=pltpu.CompilerParams(
            collective_id=0, has_side_effects=True, vmem_limit_bytes=62 << 20
        ),
    )(
        tokens[0], cotangent[0], span_ids[0], gain_one[None], gain_two[None], b_out[None], b_down[None],
        b_up[None], pack,
    )
    result, d_tokens, grads, g1, g2, bo, bd, bu = out
    small = [g1[0], bo[0], g2[0], bu[0], bd[0]]
    if sub > 1:
        grads = lax.psum_scatter(grads, "dp", scatter_dimension=0, tiled=True, axis_index_groups=groups)
        small = [v for v in lax.psum(tuple(small), "dp", axis_index_groups=groups)]
    n = grads.shape[0]
    return (
        result[None],
        d_tokens[None],
        small[0],
        grads[:, :QW].reshape(n, 3, H2W),
        grads[:, QW:QW + H2W].T,
        small[1],
        small[2],
        grads[:, QW + H2W:QW + H2W + F2],
        small[3],
        grads[:, QW + H2W + F2:].T,
        small[4],
    )


def solution(mesh):
    in_specs = (
        P("dp", "tensor", None),
        P("dp", "tensor", None),
        P("dp", None, None),
        P(),
        P("dp", None, "tensor"),
        P("tensor", "dp"),
        P(),
        P(),
        P("dp", "tensor"),
        P("tensor"),
        P("tensor", "dp"),
        P(),
    )
    out_specs = (
        P("dp", "tensor", None),
        P("dp", "tensor", None),
        P(),
        P("dp", None, "tensor"),
        P("tensor", "dp"),
        P(),
        P(),
        P("dp", "tensor"),
        P(),
        P("tensor", "dp"),
        P(),
    )
    return jax.shard_map(shards, mesh=mesh, in_specs=in_specs, out_specs=out_specs, check_vma=False)
```

time: 723 us -> 155 us (0.21); the launches traced: 713 us -> 154 us
  waiting for transfers between devices: 391 us -> 0 us
  Pallas kernels: 0 us -> 140 us
  blocking collectives: 125 us -> 0 us
  matrix products: 112 us -> 0 us
  other arithmetic: 34.3 us -> 1.53 us
  local copies, waits for them, and re-layouts: 32.8 us -> 11.8 us
  between operations: 16 us -> 0.69 us
    reduce_scatter x8 -> x0, waiting for transfers between devices: 274 us -> none  [the longest x1 77.7 us: shards(): lax.psum_scatter(grad_up, 'dp', scatter_dimension=0, tiled=True)]
    pallas_call x0 -> x1, Pallas kernels: none -> 140 us  [shards(): pl.pallas_call(functools.partial(kernel, s), out_shape=(jax.ShapeDtypeStr...]
    all_gather x6 -> x0, waiting for transfers between devices: 115 us -> none  [the longest x1 49.1 us: shards(): lax.all_gather(w_down, 'dp', axis=1, tiled=True)]
    dot_general x78 -> x0, matrix products: 112 us -> none  [the longest x1 10.5 us: shards(): jnp.dot(rows_two, up_whole, preferred_element_type=jnp.float32) + bias_whole]
    all_gather x2 -> x0, blocking collectives: 84 us -> none  [the longest x1 47 us: shards(): lax.all_gather(w_qkv, 'dp', axis=0, tiled=True)]
    psum x1 -> x0, blocking collectives: 40.7 us -> none  [shards(): lax.psum((gain_one_part, gain_two_part, jnp.sum(grad_branch, axis=0, dtyp...]
    reduce_sum x17 -> x0, other arithmetic: 17.2 us -> none  [the longest x2 5.57 us: normalize_back(): jnp.sum(incoming_grad * unit_rows, axis=0)]
    unnamed x59 -> x23, local copies, waits for them, and re-layouts: 15.7 us -> 6.35 us
  transfers between devices with their start and end apart: 14 -> 0, of which waited for: 12 -> 0; matrix products, arithmetic and copies ran while one was open for 15% -> 0% of each run, Pallas kernels for 0% -> 0%
where the time goes in v1:
time: 155 us; the launch traced here: 154 us
  Pallas kernels  140 us (90%)
  local copies, waits for them, and re-layouts  11.8 us (8%)
    pallas_call x1, Pallas kernels, shards(): pl.pallas_call(functools.partial(kernel, s), out_shape=(jax.ShapeDtypeStr...  140 us
    unnamed x23, local copies, waits for them, and re-layouts  6.35 us

profile of v1, /device:TPU:0, one launch (start us, length us, event | category | flops | bytes accessed | tf_op | source)
XLA Modules:
  0.0 154.4 jit_solution(12002469329743419927)
XLA Ops:
  0.6 0.0 copy-start.1
  0.7 0.0 copy-start.2
  0.7 0.8 copy.28
  1.5 0.0 copy-done.1
  1.5 0.0 copy-done.2
  1.5 1.5 pad_maximum_fusion.refs_8_
  3.0 140.4 %shard_map.203 = (bf16[1024,512]{1,0:T(8,128)(2,1)}, bf16[1024,512]{1,0:T(8,128)(2,1)}, f32[32,3072]{1,0:T(8,128)}, f32[1,512]{1,0:T(1,128)}, f32[1,512]{1,0:T(1...) custom-call(bf16[1024,512]{1,0:T(8,128)(2,1)} %bitcast.27, bf16[1024,512]{1,0:T(8,128)(2,1)} %bitcast.28, ...), custom_call_target="tpu_custom_call" | custom-call | tf_op jit(solution)/shard_map/pallas_call | solution.py:630
  143.5 1.4 slice_bitcast_fusion.1
  144.9 0.9 slice.12
  145.8 1.7 %slice_bitcast_fusion = (f32[1024,32]{0,1:T(8,128)}, f32[32,1024]{1,0:T(8,128)}) fusion(f32[32,3072]{1,0:T(8,128)} %get-tuple-element.22), kind=kLoop, calls=%fused_computation.1 | loop fusion | bytes 524288 | tf_op jit(solution)/shard_map/transpose | solution.py:710
  147.4 0.6 copy.30
  148.1 0.0 copy-start
  148.1 2.4 %copy.38 = bf16[1,1024,512]{2,1,0:T(8,128)(2,1)} copy(bf16[1,1024,512]{2,1,0:T(8,128)(2,1)} %bitcast.30) | data formatting | bytes 2097152
  150.4 0.0 copy-done
  150.4 0.0 copy-start.7
  150.5 0.0 copy-start.6
  150.5 0.0 copy-start.5
  150.5 1.0 copy.39
  151.4 0.0 copy-done.7
  151.4 0.0 copy-start.3
  151.4 0.6 copy.40
  152.0 0.0 copy-done.6
  152.0 0.6 copy.41
  152.6 0.0 copy-done.5
  152.6 0.6 copy.42
  153.2 0.0 copy-done.3
  153.2 0.0 copy-start.4
  153.2 0.6 copy.43
  153.8 0.1 copy-done.4
  153.9 0.6 copy.44
Async XLA Ops:
  0.6 0.9 copy-start.1
  0.7 0.8 copy-start.2
  148.1 2.4 %copy-start = (bf16[1024,512]{1,0:T(8,128)(2,1)S(1)}, bf16[1024,512]{1,0:T(8,128)(2,1)}, u32[]{:S(2)}) copy-start(bf16[1024,512]{1,0:T(8,128)(2,1)} %get-tuple-element.20) | copy-start | bytes 3145732
  150.4 1.0 copy-start.7
  150.5 1.6 %copy-start.6 = (f32[1,512]{1,0:T(1,128)S(1)}, f32[1,512]{1,0:T(1,128)}, u32[]{:S(2)}) copy-start(f32[1,512]{1,0:T(1,128)} %get-tuple-element.23) | copy-start | bytes 6148
  150.5 2.1 %copy-start.5 = (f32[1,512]{1,0:T(1,128)S(1)}, f32[1,512]{1,0:T(1,128)}, u32[]{:S(2)}) copy-start(f32[1,512]{1,0:T(1,128)} %get-tuple-element.24) | copy-start | bytes 6148
  151.4 1.7 %copy-start.3 = (f32[1,2048]{1,0:T(1,128)S(1)}, f32[1,2048]{1,0:T(1,128)}, u32[]{:S(2)}) copy-start(f32[1,2048]{1,0:T(1,128)} %get-tuple-element.25) | copy-start | bytes 24580
  153.2 0.7 copy-start.4

commit v2 on v1

v2 whole, which is shorter than its diff:
```python
import functools
import math

import jax
import jax.numpy as jnp
from jax import lax
from jax.experimental import pallas as pl
from jax.experimental.pallas import tpu as pltpu
from jax.sharding import PartitionSpec as P

HD = 64
BLK = 256
EPS = 1e-05
MASKED = -1e30
Z = 4
YX = 4
GROUPS = Z * YX
F32 = jnp.float32
BF = jnp.bfloat16
MESH = pl.DeviceIdType.MESH


def dot(a, b, ca, cb):
    return lax.dot_general(a, b, (((ca,), (cb,)), ((), ())), preferred_element_type=F32)


def nn(a, b):
    return dot(a, b, 1, 0)


def nt(a, b):
    return dot(a, b, 1, 1)


def tn(a, b):
    return dot(a, b, 0, 0)


def iota(shape, axis):
    return lax.broadcasted_iota(jnp.int32, shape, axis)


def unit_rows(values):
    centre = values - jnp.mean(values, axis=-1, keepdims=True)
    spread = jnp.mean(centre * centre, axis=-1, keepdims=True)
    inverse = lax.rsqrt(spread + EPS)
    return centre * inverse, inverse


def eight(values):
    return jnp.sum(values.reshape(values.shape[0] // 8, 8, values.shape[1]), axis=0)


class Sizes:
    pass


def kernel(s, *refs):
    (tok_in, cot_in, span, gain1, gain2, bout, bdown, bup_own, s_qkv, s_out, s_up, s_dn) = refs[:12]
    (res_out, dtok_out, g_qkv, g_out, g_up, g_dn, o_gain1, o_gain2, o_bout, o_bdown, o_bup) = refs[12:23]
    (W, G, R0, R1, R2, R3, H1, H1T, QKV, PT, PF, O, MID, H2, H2T, COTT, HID, GI, GB, GBT,
     BUP, KSV, KB, VB, DKS, DVS, DSV, DSVR, SHARE, SPC, M8, BUACC, ACC, SM, SMR, tok, cot, RES, GO,
     ag_s, ag_r, rs_s, rs_r, sx_s, sx_r, lc, oc) = refs[23:]
    D, H2W, F2, NB = s.D, s.H2W, s.F2, s.NB
    QW = 3 * H2W
    FC, NFC = s.FC, F2 // s.FC
    C_OUT = QW

    def c_up(fc):
        return QW + H2W + 2 * FC * fc

    def c_dn(fc):
        return QW + H2W + 2 * FC * fc + FC

    d = lax.axis_index("dp")
    t = lax.axis_index("tensor")
    g = d // s.sub
    z = g // YX
    yx = g % YX
    rest = d % s.sub
    b2 = 2 - t
    b3 = 1 + t

    def at(zz, q):
        return ((zz * YX + q) * s.sub + rest, t)

    def flip(q, bit):
        y_bit, x_bit = q // 2, q % 2
        return jnp.where(bit == 2, (1 - y_bit) * 2 + x_bit, y_bit * 2 + 1 - x_bit)

    yx2 = flip(yx, b2)
    yx3 = flip(yx, b3)
    yx23 = 3 - yx
    pair = (d, 1 - t)
    peer2 = at(z, yx2)
    peer3 = at(z, yx3)
    zpeers = [at((z + k) % Z, yx) for k in range(1, Z)]

    barrier = pltpu.get_barrier_semaphore()
    for who in [pair, peer2, peer3] + zpeers:
        pl.semaphore_signal(barrier, inc=1, device_id=who, device_id_type=MESH)

    fetches = []

    def fetch(src, dst):
        cp = pltpu.make_async_copy(src, dst, lc.at[len(fetches)])
        cp.start()
        fetches.append(cp)

    own = W.at[t, z, yx]
    for j in range(3):
        for pr in range(2):
            fetch(s_qkv.at[j, :, pl.ds(128 * pr, 128)], own.at[:, pl.ds(384 * pr + 128 * j, 128)])
    fetch(s_out, own.at[:, pl.ds(C_OUT, H2W)])
    for fc in range(NFC):
        fetch(s_up.at[:, pl.ds(fc * FC, FC)], own.at[:, pl.ds(c_up(fc), FC)])
        fetch(s_dn.at[:, pl.ds(fc * FC, FC)], own.at[:, pl.ds(c_dn(fc), FC)])
    n_shards = len(fetches)
    fetch(tok_in, tok)
    fetch(cot_in, cot)
    BUP[t] = jnp.broadcast_to(bup_own[...], (8, F2))

    half_rows = iota((8, BLK), 0)
    for b in range(NB):
        line = span[pl.ds(t * NB + b, 1), :]
        belongs = jnp.logical_and(half_rows // NB == line, half_rows % NB == b)
        M8[:, b * BLK:(b + 1) * BLK] = belongs.astype(F32)
    SPC[...] = jnp.concatenate([span[...].astype(F32), jnp.zeros((120, BLK), F32)], axis=0).T
    zeros_in = (span[...] == 0).astype(F32)
    ones_in = (span[...] == 1).astype(F32)
    n_zero = jnp.sum(zeros_in, axis=1, keepdims=True)
    n_one = jnp.sum(ones_in, axis=1, keepdims=True)
    counts = jnp.concatenate(
        [n_zero[:NB], n_one[:NB], n_zero[NB:2 * NB], n_one[NB:2 * NB]], axis=0
    )
    log_counts = jnp.concatenate([jnp.log(counts)] * 4, axis=0)
    own_counts = jnp.sum(M8[...], axis=1, keepdims=True)
    code = iota((64, 1), 0) % 16
    block_of = (code // 8) * NB + code % NB

    for cp in fetches[:n_shards]:
        cp.wait()
    pl.semaphore_wait(barrier, 3 + Z - 1)

    def remote(src, dst, ss, rs, who):
        return pltpu.make_async_remote_copy(
            src_ref=src, dst_ref=dst, send_sem=ss, recv_sem=rs, device_id=who, device_id_type=MESH
        )

    chunks = s.ag_chunks
    group_of = {"o": yx, "2": yx2, "3": yx3, "23": yx23}
    kinds = ["z1", "z2", "z3"] + [a + str(k) for a in ("2s", "3s", "3t") for k in range(Z)]
    kinds += ["p" + a + "_" + str(k) for a in group_of for k in range(Z)]
    number = {kind: i for i, kind in enumerate(kinds)}

    def ag_copy(c, kind, got=False):
        lo, n = chunks[c]
        cols = pl.ds(lo, n)
        if kind[0] == "z":
            k = int(kind[1])
            window, who = W.at[t, (z + Z - k) % Z if got else z, yx, :, cols], zpeers[k - 1]
        elif kind[0] == "p":
            name, k = kind[1:].split("_")
            window, who = W.at[1 - t if got else t, (z + Z - int(k)) % Z, group_of[name], :, cols], pair
        else:
            there, here, who = {"2s": (yx2, yx, peer2), "3s": (yx3, yx, peer3), "3t": (yx23, yx2, peer3)}[kind[:2]]
            window = W.at[t, (z + Z - int(kind[2])) % Z, there if got else here, :, cols]
        i = number[kind]
        return remote(window, window, ag_s.at[c, i], ag_r.at[c, i], who)

    def ag_event(event):
        c, got, starts = event
        if got is not None:
            ag_copy(c, got, True).wait_recv()
        for kind in starts:
            ag_copy(c, kind).start()

    def ag_done(c):
        for name in group_of:
            for k in range(Z):
                ag_copy(c, "p" + name + "_" + str(k), True).wait_recv()

    order = (1, 3, 2)
    after = (0, 1, 3, 2)

    def ag_events(c):
        first = [(c, None, ["z1", "z3", "z2", "2s0", "3s0", "po_0"])]
        second = [(c, f"z{k}", [f"2s{k}", f"3s{k}", f"po_{k}"]) for k in order]
        third = [(c, f"2s{k}", [f"3t{k}", f"p2_{k}"]) for k in after]
        fourth = [(c, f"3s{k}", [f"p3_{k}"]) for k in after]
        fifth = [(c, f"3t{k}", [f"p23_{k}"]) for k in after]
        return [first, second, third, fourth, fifth]

    gathers = [sum(ag_events(c), []) for c in range(len(chunks))]

    def run(events):
        for kind, c, step in events:
            if kind == "a":
                ag_event(gathers[c][step])
            elif kind == "r":
                rs_steps[step](c)
            else:
                small_step(step)

    def in_slots(i, places):
        for when, events in enumerate(places):
            if events:
                @pl.when(i == when)
                def _():
                    run(events)

    def small_copy(i, src, dst, who):
        return remote(src, dst, sx_s.at[i], sx_r.at[i], who)

    def exchange(i, who):
        return small_copy(4 + i, SM.at[i], SMR.at[i], who)

    def small_step(i):
        whos = (pair, peer3, peer2)
        if i > 0:
            exchange(i - 1, whos[i - 1]).wait_recv()
            SM[i] = SM[i - 1] + SMR[i - 1]
        if i < 3:
            exchange(i, whos[i]).start()
        else:
            SMR[3 + z] = SM[3]
            for k in range(1, Z):
                small_copy(6 + k, SM.at[3], SMR.at[3 + z], zpeers[k - 1]).start()

    run(s.plan["first"])
    bup_copy = small_copy(0, BUP.at[t], BUP.at[t], pair)
    bup_copy.start()

    def wl(half, lo, n):
        return W[half, :, :, :, pl.ds(lo, n)].reshape(D, n)

    def rows_of(b):
        return pl.ds(pl.multiple_of(b * BLK, BLK), BLK)

    for cp in fetches[n_shards:]:
        cp.wait()

    def norm_one(b, _):
        r = rows_of(b)
        unit, _inv = unit_rows(tok[r, :].astype(F32))
        low = (unit * gain1[...]).astype(BF)
        H1[r, :] = low
        H1T[:, r] = low.T
        COTT[:, r] = cot[r, :].T
        return 0

    lax.fori_loop(0, NB, norm_one, 0)

    BUACC[...] = jnp.zeros_like(BUACC)
    ACC[...] = jnp.zeros_like(ACC)
    DKS[...] = jnp.zeros_like(DKS)
    DVS[...] = jnp.zeros_like(DVS)

    run(s.plan["second"])
    ag_done(0)

    q_scale = jnp.where(iota((1, QW), 1) % 384 < 128, 1.0 / math.sqrt(HD), 1.0).astype(F32)

    def project(i, _):
        b, half = i // 2, i % 2
        r = rows_of(b)
        y = nn(H1[r, :], wl(half, 0, QW)) * q_scale
        QKV[half, r, :] = y.astype(BF)
        in_slots(i, s.plan["project"])
        return 0

    lax.fori_loop(0, 2 * NB, project, 0)

    member_low = jnp.concatenate([M8[...], M8[...]], axis=0).astype(BF)
    for half in range(2):
        for pr in range(2):
            sums = nn(member_low, QKV[half, :, 384 * pr + 128:384 * pr + 384])[:8]
            means = (sums / own_counts).astype(BF).astype(F32)
            for kind in range(2):
                lo = (2 * half + kind) * H2W + 128 * pr
                KSV[t, :, lo:lo + 128] = means[:, 128 * kind:128 * kind + 128]
    ksv_copy = small_copy(1, KSV.at[t], KSV.at[t], pair)
    ksv_copy.start()
    run(s.plan["third"])
    small_copy(1, KSV.at[1 - t], KSV.at[1 - t], pair).wait_recv()
    diagonal = iota((64, H2W), 0) // 16 == iota((64, H2W), 1) // HD
    everything = KSV[...].reshape(16, 4 * H2W)
    for half in range(2):
        for kind, out in ((0, KB), (1, VB)):
            lo = (2 * half + kind) * H2W
            tiled = jnp.concatenate([everything[:, lo:lo + H2W]] * 4, axis=0)
            out[half] = jnp.where(diagonal, tiled, 0.0).astype(BF)

    even = iota((BLK, 128), 1) < HD

    def head_only(values, e):
        return jnp.where(even if e == 0 else jnp.logical_not(even), values, jnp.zeros_like(values))

    def attend(i, _):
        b, half = i // 2, i % 2
        r = rows_of(b)
        q = jnp.concatenate([QKV[half, r, 0:128], QKV[half, r, 384:512]], axis=1)
        far = nt(KB[half], q) + log_counts
        far = jnp.where(block_of < t * NB + b, far, MASKED)
        parts, far_parts = [], []
        for pr in range(2):
            lanes = slice(pr * 128, (pr + 1) * 128)
            q2 = q[:, lanes]
            k2 = QKV[half, r, pr * 384 + 128:pr * 384 + 256]
            v2 = QKV[half, r, pr * 384 + 256:pr * 384 + 384]
            both = []
            for e in range(2):
                hl = 2 * pr + e
                near = nt(k2, head_only(q2, e))
                sf = far[16 * hl:16 * hl + 16]
                largest = jnp.maximum(
                    jnp.max(near, axis=0, keepdims=True), jnp.max(sf, axis=0, keepdims=True)
                )
                pn = jnp.exp(near - largest)
                pf = jnp.exp(sf - largest)
                total = jnp.sum(pn, axis=0, keepdims=True) + jnp.sum(pf, axis=0, keepdims=True)
                inv = 1.0 / total
                pn = (pn * inv).astype(BF)
                PT[half, b, hl] = pn
                far_parts.append(pf * inv)
                both.append(tn(pn, v2))
            parts.append(jnp.where(even, both[0], both[1]))
        pf_all = jnp.concatenate(far_parts, axis=0).astype(BF)
        PF[half, b] = pf_all
        out = jnp.concatenate(parts, axis=1) + tn(pf_all, VB[half])
        O[half, r, :] = out.astype(BF)
        in_slots(i, s.plan["attend"])
        return 0

    lax.fori_loop(0, 2 * NB, attend, 0)

    run(s.plan["proj_wait"])
    ag_done(1)
    small_copy(0, BUP.at[1 - t], BUP.at[1 - t], pair).wait_recv()

    def out_proj(b, _):
        r = rows_of(b)
        branch = nt(O[0, r, :], wl(0, C_OUT, H2W)) + nt(O[1, r, :], wl(1, C_OUT, H2W))
        middle = tok[r, :].astype(F32) + (branch + bout[...])
        MID[r, :] = middle
        unit, _inv = unit_rows(middle)
        low = (unit * gain2[...]).astype(BF)
        H2[r, :] = low
        H2T[:, r] = low.T
        in_slots(b, s.plan["proj"])
        return 0

    lax.fori_loop(0, NB, out_proj, 0)

    c0 = math.sqrt(2.0 / math.pi)
    c1 = c0 * 0.044715

    def feed(fc):
        def one(i, _):
            b, half = i // 2, i % 2
            r = rows_of(b)
            cols = slice(fc * FC, (fc + 1) * FC)
            x = nn(H2[r, :], wl(half, c_up(fc), FC)) + BUP[half, 0:1, cols]
            gh = nn(cot[r, :], wl(half, c_dn(fc), FC))
            sq = x * x
            th = jnp.tanh(x * (c0 + c1 * sq))
            up = 0.5 + 0.5 * th
            HID[half, r, cols] = (x * up).astype(BF)
            slope = up + (0.5 * x) * (1.0 - th * th) * (c0 + (3.0 * c1) * sq)
            gi = gh * slope
            GI[half, r, cols] = gi.astype(BF)
            BUACC[half, :, cols] += eight(gi)
            in_slots(i, s.plan["feed" + str(fc)])
            return 0

        lax.fori_loop(0, 2 * NB, one, 0)

    def over_units(values, r, place):
        total = None
        for half in range(2):
            for fc in range(NFC):
                part = nt(values[half, r, fc * FC:(fc + 1) * FC], wl(half, place(fc), FC))
                total = part if total is None else total + part
        return total

    def feed_back(b, _):
        r = rows_of(b)
        middle = MID[r, :]
        RES[r, :] = middle
        g2 = over_units(GI, r, c_up)
        unit, inverse = unit_rows(middle)
        e = g2 * gain2[...]
        m1 = jnp.mean(e, axis=-1, keepdims=True)
        m2 = jnp.mean(e * unit, axis=-1, keepdims=True)
        grad_out = cot[r, :].astype(F32)
        mid = grad_out + inverse * (e - m1 - unit * m2)
        MID[r, :] = mid
        low = mid.astype(BF)
        GB[r, :] = low
        GBT[:, r] = low.T
        for half in range(2):
            GO[half, r, :] = nn(low, wl(half, C_OUT, H2W)).astype(BF)
        ACC[1] += eight(g2 * unit)
        ACC[2] += eight(mid)
        ACC[3] += eight(grad_out)
        in_slots(b, s.plan["feed_back"])
        return 0

    def give(b, _):
        r = rows_of(b)
        H1[r, :] = (RES[r, :] + (over_units(HID, r, c_dn) + bdown[...])).astype(BF)
        in_slots(b, s.plan["give"])
        return 0

    rchunks = s.rs_chunks

    def rs_copy(c, kind):
        lo, n = rchunks[c]
        cols = pl.ds(lo, n)
        if kind == 0:
            src, dst, who = G.at[1 - t, :, :, :, cols], R0.at[:, :, :, cols], pair
        elif kind == 1:
            src, dst, who = G.at[t, :, yx3, :, cols], R1.at[0, :, :, cols], peer3
        elif kind == 2:
            src, dst, who = G.at[t, :, yx23, :, cols], R1.at[1, :, :, cols], peer3
        elif kind == 3:
            src, dst, who = G.at[t, :, yx2, :, cols], R2.at[:, :, cols], peer2
        else:
            k = kind - 3
            src, dst, who = G.at[t, (z + k) % Z, yx, :, cols], R3.at[k - 1, :, cols], zpeers[k - 1]
        return remote(src, dst, rs_s.at[c, kind], rs_r.at[c, kind], who)

    def rs0(c):
        rs_copy(c, 0).start()

    def rs1(c):
        lo, n = rchunks[c]
        rs_copy(c, 0).wait_recv()
        cols = pl.ds(lo, n)

        def add(q):
            for zz in range(Z):
                G[t, zz, q, :, cols] = (
                    G[t, zz, q, :, cols].astype(F32) + R0[zz, q, :, cols].astype(F32)
                ).astype(BF)

        add(yx23)
        rs_copy(c, 2).start()
        add(yx3)
        rs_copy(c, 1).start()
        add(yx2)
        add(yx)

    def rs2(c):
        lo, n = rchunks[c]
        cols = pl.ds(lo, n)

        def add(q, j):
            for zz in range(Z):
                G[t, zz, q, :, cols] = (
                    G[t, zz, q, :, cols].astype(F32) + R1[j, zz, :, cols].astype(F32)
                ).astype(BF)

        rs_copy(c, 2).wait_recv()
        add(yx2, 1)
        rs_copy(c, 3).start()
        rs_copy(c, 1).wait_recv()
        add(yx, 0)

    def rs3(c):
        lo, n = rchunks[c]
        cols = pl.ds(lo, n)
        rs_copy(c, 3).wait_recv()
        for zz in range(Z):
            G[t, zz, yx, :, cols] = (
                G[t, zz, yx, :, cols].astype(F32) + R2[zz, :, cols].astype(F32)
            ).astype(BF)
        for kind in (4, 5, 6):
            rs_copy(c, kind).start()

    def rs4(c):
        lo, n = rchunks[c]
        cols = pl.ds(lo, n)
        total = G[t, z, yx, :, cols].astype(F32)
        for kind in (4, 5, 6):
            rs_copy(c, kind).wait_recv()
            total = total + R3[kind - 4, :, cols].astype(F32)
        total = total * s.factor
        if lo < QW:
            for j in range(3):
                g_qkv[j, :, lo // 3:lo // 3 + 128] = total[:, 128 * j:128 * j + 128]
        elif lo == C_OUT:
            g_out[...] = total
        else:
            for part in range(n // FC):
                place = (lo - QW - H2W) // FC + part
                dst = g_dn if place % 2 else g_up
                dst[:, (place // 2) * FC:(place // 2 + 1) * FC] = total[:, part * FC:(part + 1) * FC]

    rs_steps = (rs0, rs1, rs2, rs3, rs4)

    def weight_grad(lhs, rhs, lo, c_lo, n):
        def one(half, _):
            y = nn(lhs[...], rhs[half, :, pl.ds(lo, n)]).astype(BF)
            G[half, :, :, :, pl.ds(c_lo, n)] = y.reshape(Z, YX, D // GROUPS, n)
            return 0

        lax.fori_loop(0, 2, one, 0)

    for fc in range(NFC):
        if fc == NFC - 1:
            run(s.plan["feed1_wait"])
            ag_done(2)
        feed(fc)
        weight_grad(H2T, GI, fc * FC, c_up(fc), FC)
        run(s.plan["w" + str(2 * fc)])
        weight_grad(COTT, HID, fc * FC, c_dn(fc), FC)
        run(s.plan["w" + str(2 * fc + 1)])

    lax.fori_loop(0, NB, feed_back, 0)
    weight_grad(GBT, O, 0, C_OUT, H2W)
    run(s.plan["out"])

    GP = GI
    halves = iota((32, 128), 0) // 16 == iota((32, 128), 1) // HD

    def attend_back(pr):
        lo = 384 * pr

        def one(i, _):
            b, half = i // 2, i % 2
            r = rows_of(b)
            q2 = QKV[half, r, lo:lo + 128]
            k2 = QKV[half, r, lo + 128:lo + 256]
            v2 = QKV[half, r, lo + 256:lo + 384]
            do2 = GO[half, r, 128 * pr:128 * pr + 128]
            means_k = KB[half, 32 * pr:32 * pr + 32, 128 * pr:128 * pr + 128]
            means_v = VB[half, 32 * pr:32 * pr + 32, 128 * pr:128 * pr + 128]
            pf_low = PF[half, b, 32 * pr:32 * pr + 32]
            dpf = nt(means_v, do2)
            pf_all = pf_low.astype(F32)
            far_parts, dqs, dks, dvs = [], [], [], []
            for e in range(2):
                dp = nt(v2, head_only(do2, e))
                p_low = PT[half, b, 2 * pr + e]
                p = p_low.astype(F32)
                df = dpf[16 * e:16 * e + 16]
                pf = pf_all[16 * e:16 * e + 16]
                corr = jnp.sum(p * dp, axis=0, keepdims=True) + jnp.sum(pf * df, axis=0, keepdims=True)
                ds = (p * (dp - corr)).astype(BF)
                far_parts.append(pf * (df - corr))
                dqs.append(tn(ds, k2))
                dks.append(nn(ds, q2))
                dvs.append(nn(p_low, do2))
            dsf = jnp.concatenate(far_parts, axis=0).astype(BF)
            dq = (jnp.where(even, dqs[0], dqs[1]) + tn(dsf, means_k)) * (1.0 / math.sqrt(HD))
            GP[half, r, lo:lo + 128] = dq.astype(BF)
            GP[half, r, lo + 128:lo + 256] = jnp.where(even, dks[0], dks[1]).astype(BF)
            GP[half, r, lo + 256:lo + 384] = jnp.where(even, dvs[0], dvs[1]).astype(BF)
            DKS[half, pr] += nn(dsf, q2)
            DVS[half, pr] += nn(pf_low, do2)
            in_slots(i, s.plan["back" + str(pr)])
            return 0

        lax.fori_loop(0, 2 * NB, one, 0)

        for half in range(2):
            for kind, src in ((0, DKS), (1, DVS)):
                kept = jnp.where(halves, src[half, pr], 0.0)
                at_lane = (2 * half + kind) * 128
                DSV[pr, :, :, at_lane:at_lane + 128] = (kept[0:16] + kept[16:32]).reshape(2, 8, 128)
        small_copy(2 + pr, DSV.at[pr, 1 - t], DSVR.at[pr], pair).start()
        run(s.plan["share" + str(pr)])
        small_copy(2 + pr, DSV.at[pr, 1 - t], DSVR.at[pr], pair).wait_recv()
        SHARE[pr] = (DSV[pr, t] + DSVR[pr]) / own_counts

        def spread(b, _):
            r = rows_of(b)
            column = jnp.sum(jnp.where(span_lane == t * NB + b, SPC[...], 0.0), axis=1, keepdims=True)
            for half in range(2):
                lanes = slice(256 * half, 256 * half + 256)
                shared = jnp.where(
                    column == 0.0, SHARE[pr, pl.ds(b, 1), lanes], SHARE[pr, pl.ds(NB + b, 1), lanes]
                )
                GP[half, r, lo + 128:lo + 384] = (GP[half, r, lo + 128:lo + 384].astype(F32) + shared).astype(BF)
            return 0

        lax.fori_loop(0, NB, spread, 0)
        run(s.plan["spread" + str(pr)])
        weight_grad(H1T, GP, lo, lo, 384)
        run(s.plan["q" + str(pr)])

    span_lane = iota((BLK, 128), 1)
    attend_back(0)
    attend_back(1)

    def last(b, _):
        r = rows_of(b)
        grad = nt(GP[0, r, 0:QW], wl(0, 0, QW)) + nt(GP[1, r, 0:QW], wl(1, 0, QW))
        unit, inverse = unit_rows(tok[r, :].astype(F32))
        e = grad * gain1[...]
        m1 = jnp.mean(e, axis=-1, keepdims=True)
        m2 = jnp.mean(e * unit, axis=-1, keepdims=True)
        H2[r, :] = (MID[r, :] + inverse * (e - m1 - unit * m2)).astype(BF)
        ACC[0] += eight(grad * unit)
        in_slots(b, s.plan["last"])
        return 0

    lax.fori_loop(0, NB, last, 0)
    out_copies = [pltpu.make_async_copy(H2, dtok_out, oc.at[0]), pltpu.make_async_copy(H1, res_out, oc.at[1])]
    out_copies[0].start()

    folded = [jnp.sum(ACC[j], axis=0, keepdims=True) for j in range(4)]
    for half in range(2):
        line = jnp.sum(BUACC[half], axis=0, keepdims=True)
        folded += [line[:, j * D:(j + 1) * D] for j in range(F2 // D)]
    SM[0] = jnp.concatenate(folded, axis=0)

    run(s.plan["small"])
    lax.fori_loop(0, NB, give, 0)
    out_copies[1].start()
    run(s.plan["end"])
    for k in range(1, Z):
        small_copy(6 + k, SM.at[3], SMR.at[3 + (z + Z - k) % Z], zpeers[k - 1]).wait_recv()
    summed = (SMR[3] + SMR[4] + SMR[5] + SMR[6]) * s.factor
    o_gain1[...] = summed[0:1]
    o_gain2[...] = summed[1:2]
    o_bout[...] = summed[2:3]
    o_bdown[...] = summed[3:4]
    for j in range(2 * F2 // D):
        o_bup[:, j * D:(j + 1) * D] = summed[4 + j:5 + j]


    for cp in out_copies:
        cp.wait()
    for c in range(len(chunks)):
        for kind in kinds:
            ag_copy(c, kind).wait_send()
    for c in range(len(rchunks)):
        for kind in range(7):
            rs_copy(c, kind).wait_send()
    bup_copy.wait_send()
    ksv_copy.wait_send()
    for pr in range(2):
        small_copy(2 + pr, DSV.at[pr, 1 - t], DSVR.at[pr], pair).wait_send()
    for i, who in enumerate((pair, peer3, peer2)):
        exchange(i, who).wait_send()
    for k in range(1, Z):
        small_copy(6 + k, SM.at[3], SMR.at[3 + z], zpeers[k - 1]).wait_send()


def deliver(n, *refs):
    ins, outs, held, (got, sent) = refs[:n], refs[n:2 * n], refs[2 * n:3 * n], refs[3 * n:]
    firsts = [pltpu.make_async_copy(ins[i], held[i], got.at[i]) for i in range(n)]
    seconds = [pltpu.make_async_copy(held[i], outs[i], sent.at[i]) for i in range(n)]
    for cp in firsts:
        cp.start()
    for first, second in zip(firsts, seconds):
        first.wait()
        second.start()
    for cp in seconds:
        cp.wait()


def shards(
    tokens, cotangent, span_ids, gain_one, w_qkv, w_out, b_out, gain_two, w_up, b_up, w_down, b_down
):
    s = Sizes()
    dp = lax.axis_size("dp")
    s.sub = dp // GROUPS
    s.D = tokens.shape[2]
    s.rows = tokens.shape[1]
    s.NB = s.rows // BLK
    s.H2W = w_qkv.shape[2]
    s.F2 = w_up.shape[1]
    s.factor = 1.0 / math.sqrt(dp * lax.axis_size("tensor") * s.rows)
    sub, D, H2W, F2, N, NB = s.sub, s.D, s.H2W, s.F2, s.rows, s.NB
    QW = 3 * H2W
    width = QW + H2W + 2 * F2
    s.FC = 512
    s.FC = 512
    s.ag_chunks = [(0, 768), (768, 1280), (2048, 1024)]
    s.rs_chunks = [(1024, 512), (1536, 512), (2048, 512), (2560, 512), (768, 256), (0, 384), (384, 384)]
    s.plan = {
        "first": (('a', 0, 0), ),
        "second": (('a', 0, 4), ('a', 0, 8), ('a', 0, 1), ('a', 0, 12), ('a', 0, 2), ('a', 0, 5), ('a', 0, 9), ('a', 0, 3), ('a', 1, 0), ('a', 0, 6), ('a', 0, 10), ('a', 0, 13), ('a', 0, 7), ('a', 0, 11), ('a', 1, 4), ('a', 1, 8), ('a', 1, 1), ('a', 0, 14), ('a', 0, 15), ('a', 1, 2), ('a', 1, 12), ),
        "third": (('a', 1, 13), ),
        "proj_wait": (),
        "feed1_wait": (),
        "w0": (('r', 0, 0), ),
        "w1": (('r', 1, 0), ),
        "w2": (('r', 2, 0), ),
        "w3": (('r', 3, 0), ('r', 1, 2), ),
        "out": (('r', 4, 0), ('r', 2, 2), ),
        "share0": (),
        "spread0": (('r', 4, 3), ('r', 2, 4), ),
        "q0": (('r', 5, 0), ),
        "share1": (),
        "spread1": (('r', 5, 3), ),
        "q1": (('r', 6, 0), ),
        "small": (('s', 0, 0), ),
        "end": (('r', 6, 2), ('s', 0, 2), ('r', 6, 3), ('s', 0, 3), ('r', 6, 4), ),
        "project": (
            (),
            (('a', 1, 5), ),
            (),
            (('a', 1, 9), ),
            (),
            (('a', 1, 6), ),
            (),
            (('a', 1, 3), ('a', 2, 0), ('a', 1, 10), ),
        ),
        "attend": (
            (('a', 1, 14), ('a', 1, 7), ),
            (('a', 1, 11), ),
            (('a', 2, 1), ('a', 2, 4), ),
            (('a', 2, 8), ),
            (('a', 2, 2), ('a', 1, 15), ),
            (('a', 2, 5), ),
            (('a', 2, 9), ),
            (('a', 2, 12), ('a', 2, 3), ('a', 2, 6), ),
        ),
        "proj": (
            (('a', 2, 10), ),
            (('a', 2, 13), ),
            (),
            (('a', 2, 7), ),
        ),
        "feed0": (
            (('a', 2, 11), ),
            (('a', 2, 14), ),
            (),
            (('a', 2, 15), ),
            (),
            (),
            (),
            (),
        ),
        "feed1": (
            (('r', 0, 1), ),
            (),
            (('r', 1, 1), ),
            (),
            (),
            (),
            (),
            (('r', 0, 2), ),
        ),
        "feed_back": (
            (('r', 2, 1), ('r', 0, 3), ),
            (('r', 3, 1), ),
            (('r', 1, 3), ),
            (),
        ),
        "back0": (
            (('r', 0, 4), ),
            (('r', 4, 1), ),
            (('r', 3, 2), ),
            (('r', 1, 4), ('r', 2, 3), ),
            (),
            (('r', 4, 2), ),
            (('r', 3, 3), ),
            (),
        ),
        "back1": (
            (),
            (('r', 3, 4), ('r', 5, 1), ),
            (('r', 4, 4), ),
            (),
            (),
            (('r', 5, 2), ),
            (),
            (),
        ),
        "last": (
            (),
            (),
            (('r', 6, 1), ),
            (('r', 5, 4), ),
        ),
        "give": (
            (),
            (('s', 0, 1), ),
            (),
            (),
        ),
    }
    groups = [[a * sub + b for b in range(sub)] for a in range(dp // sub)]
    pieces = [jnp.transpose(w_qkv, (1, 0, 2)), w_out.T, w_up, w_down.T]
    if sub > 1:
        pieces = [
            lax.all_gather(piece, "dp", axis=piece.ndim - 2, tiled=True, axis_index_groups=groups)
            for piece in pieces
        ]
    R = D // GROUPS

    def vm(*shape, dtype=BF):
        return pltpu.VMEM(shape, dtype)

    any_space = pl.BlockSpec(memory_space=pl.ANY)
    in_vmem = pl.BlockSpec(memory_space=pltpu.VMEM)
    results = (
        jax.ShapeDtypeStruct((N, D), BF),
        jax.ShapeDtypeStruct((N, D), BF),
        jax.ShapeDtypeStruct((3, R, H2W), F32),
        jax.ShapeDtypeStruct((R, H2W), F32),
        jax.ShapeDtypeStruct((R, F2), F32),
        jax.ShapeDtypeStruct((R, F2), F32),
        jax.ShapeDtypeStruct((1, D), F32),
        jax.ShapeDtypeStruct((1, D), F32),
        jax.ShapeDtypeStruct((1, D), F32),
        jax.ShapeDtypeStruct((1, D), F32),
        jax.ShapeDtypeStruct((1, 2 * F2), F32),
    )
    out = pl.pallas_call(
        functools.partial(kernel, s),
        out_shape=results,
        in_specs=[any_space] * 2 + [in_vmem] * 6 + [any_space] * 4,
        out_specs=[any_space] * 2 + [in_vmem] * 9,
        scratch_shapes=[
            vm(2, Z, YX, R, width),
            vm(2, Z, YX, R, width),
            vm(Z, YX, R, width),
            vm(2, Z, R, width),
            vm(Z, R, width),
            vm(Z - 1, R, width),
            vm(N, D),
            vm(D, N),
            vm(2, N, QW),
            vm(2, NB, 4, BLK, BLK),
            vm(2, NB, 64, BLK),
            vm(2, N, H2W),
            vm(N, D, dtype=F32),
            vm(N, D),
            vm(D, N),
            vm(D, N),
            vm(2, N, F2),
            vm(2, N, F2),
            vm(N, D),
            vm(D, N),
            vm(2, 8, F2, dtype=F32),
            vm(2, 8, 4 * H2W, dtype=F32),
            vm(2, 64, H2W),
            vm(2, 64, H2W),
            vm(2, 2, 32, 128, dtype=F32),
            vm(2, 2, 32, 128, dtype=F32),
            vm(2, 2, 8, 512, dtype=F32),
            vm(2, 8, 512, dtype=F32),
            vm(2, 8, 512, dtype=F32),
            vm(BLK, 128, dtype=F32),
            vm(8, N, dtype=F32),
            vm(2, 8, F2, dtype=F32),
            vm(4, 8, D, dtype=F32),
            vm(4, 8, D, dtype=F32),
            vm(7, 8, D, dtype=F32),
            vm(N, D),
            vm(N, D),
            vm(N, D, dtype=F32),
            vm(2, N, H2W),
            pltpu.SemaphoreType.DMA((len(s.ag_chunks), 31)),
            pltpu.SemaphoreType.DMA((len(s.ag_chunks), 31)),
            pltpu.SemaphoreType.DMA((len(s.rs_chunks), 7)),
            pltpu.SemaphoreType.DMA((len(s.rs_chunks), 7)),
            pltpu.SemaphoreType.DMA((10,)),
            pltpu.SemaphoreType.DMA((10,)),
            pltpu.SemaphoreType.DMA((16,)),
            pltpu.SemaphoreType.DMA((2,)),
        ],
        compiler_params=pltpu.CompilerParams(
            collective_id=0, has_side_effects=True, vmem_limit_bytes=62 << 20
        ),
    )(
        tokens[0], cotangent[0], span_ids[0], gain_one[None], gain_two[None], b_out[None], b_down[None],
        b_up[None], *pieces,
    )
    out = list(out)
    if sub > 1:
        for i in range(2, 6):
            out[i] = lax.psum_scatter(
                out[i], "dp", scatter_dimension=out[i].ndim - 2, tiled=True, axis_index_groups=groups
            )
        out[6:] = lax.psum(tuple(out[6:]), "dp", axis_index_groups=groups)
    else:
        out = pl.pallas_call(
            functools.partial(deliver, len(results)),
            out_shape=results,
            in_specs=[any_space] * len(results),
            out_specs=[any_space] * len(results),
            scratch_shapes=[pltpu.VMEM(r.shape, r.dtype) for r in results]
            + [pltpu.SemaphoreType.DMA((len(results),))] * 2,
        )(*out)
    result, d_tokens, dq, do, du, dd, g1, g2, bo, bd, bu = out
    return (
        result[None],
        d_tokens[None],
        g1[0],
        jnp.transpose(dq, (1, 0, 2)),
        do.T,
        bo[0],
        g2[0],
        du,
        bu[0],
        dd.T,
        bd[0],
    )


def solution(mesh):
    in_specs = (
        P("dp", "tensor", None),
        P("dp", "tensor", None),
        P("dp", None, None),
        P(),
        P("dp", None, "tensor"),
        P("tensor", "dp"),
        P(),
        P(),
        P("dp", "tensor"),
        P("tensor"),
        P("tensor", "dp"),
        P(),
    )
    out_specs = (
        P("dp", "tensor", None),
        P("dp", "tensor", None),
        P(),
        P("dp", None, "tensor"),
        P("tensor", "dp"),
        P(),
        P(),
        P("dp", "tensor"),
        P(),
        P("tensor", "dp"),
        P(),
    )
    return jax.shard_map(shards, mesh=mesh, in_specs=in_specs, out_specs=out_specs, check_vma=False)
```

time: 155 us -> 112 us (0.72)
  Pallas kernels: 140 us -> 111 us
  local copies, waits for them, and re-layouts: 11.8 us -> 0 us
    pallas_call x1 -> x2, Pallas kernels: 140 us -> 111 us  [the longest x1 109 us: shards(): pl.pallas_call(functools.partial(kernel, s), out_shape=results, in_specs=...]
    unnamed x23 -> x0, local copies, waits for them, and re-layouts: 6.35 us -> none
    transpose x2 -> x0, local copies, waits for them, and re-layouts: 3.06 us -> none  [the longest x1 1.68 us: shards(): grads[:, QW + H2W + F2:]]
where the time goes in v2:
time: 112 us
  Pallas kernels  111 us (99%)
    pallas_call x1, Pallas kernels, shards(): pl.pallas_call(functools.partial(kernel, s), out_shape=results, in_specs=...  109 us
    pallas_call x1, Pallas kernels, shards(): pl.pallas_call(functools.partial(deliver, len(results)), out_shape=result...  2.87 us

profile of v2, /device:TPU:0, one launch (start us, length us, event | category | flops | bytes accessed | tf_op | source)
XLA Modules:
  0.0 112.0 jit_solution(13278016447124239701)
XLA Ops:
  0.6 108.5 %shard_map.203 = (bf16[1024,512]{1,0:T(8,128)(2,1)}, bf16[1024,512]{1,0:T(8,128)(2,1)}, f32[3,32,256]{2,1,0:T(8,128)}, f32[32,256]{1,0:T(8,128)}, f32[32,1024]{1...) custom-call(bf16[1024,512]{1,0:T(8,128)(2,1)} %bitcast.21, ...), custom_call_target="tpu_custom_call" | custom-call | tf_op jit(solution)/shard_map/pallas_call | solution.py:815
  109.2 2.9 %shard_map.204 = (bf16[1024,512]{1,0:T(8,128)(2,1)}, bf16[1024,512]{1,0:T(8,128)(2,1)}, f32[3,32,256]{2,1,0:T(8,128)}, f32[32,256]{1,0:T(8,128)}, f32[32,1024]{1...) custom-call(bf16[1024,512]{1,0:T(8,128)(2,1)} %get-tuple-element.33., ...), custom_call_target="tpu_custom_call" | custom-call | tf_op jit(solution)/shard_map/pallas_call | solution.py:884

commit v3 on v2

v3 whole, which is shorter than its diff:
```python
import functools
import math

import jax
import jax.numpy as jnp
from jax import lax
from jax.experimental import pallas as pl
from jax.experimental.pallas import tpu as pltpu
from jax.sharding import PartitionSpec as P

HD = 64
BLK = 256
EPS = 1e-05
MASKED = -1e30
Z = 4
YX = 4
GROUPS = Z * YX
F32 = jnp.float32
BF = jnp.bfloat16
MESH = pl.DeviceIdType.MESH


def dot(a, b, ca, cb):
    return lax.dot_general(a, b, (((ca,), (cb,)), ((), ())), preferred_element_type=F32)


def nn(a, b):
    return dot(a, b, 1, 0)


def nt(a, b):
    return dot(a, b, 1, 1)


def tn(a, b):
    return dot(a, b, 0, 0)


def iota(shape, axis):
    return lax.broadcasted_iota(jnp.int32, shape, axis)


def unit_rows(values):
    centre = values - jnp.mean(values, axis=-1, keepdims=True)
    spread = jnp.mean(centre * centre, axis=-1, keepdims=True)
    inverse = lax.rsqrt(spread + EPS)
    return centre * inverse, inverse


def eight(values):
    return jnp.sum(values.reshape(values.shape[0] // 8, 8, values.shape[1]), axis=0)


class Sizes:
    pass


def kernel(s, *refs):
    (tok_in, cot_in, span, gain1, gain2, bout, bdown, bup_own, s_qkv, s_out, s_up, s_dn) = refs[:12]
    (res_out, dtok_out, g_qkv, g_out, g_up, g_dn, o_gain1, o_gain2, o_bout, o_bdown, o_bup) = refs[12:23]
    (W, G, R0, R1, R2, R3, H1, H1T, QKV, PT, O, MID, H2, H2T, COTT, HID, GI, GB, GBT,
     BUP, KSV, KSB, VSB, DSV, DSVR, SHARE, SPC, M8, BUACC, ACC, SM, SMR, tok, cot, RES, GO,
     ag_s, ag_r, rs_s, rs_r, sx_s, sx_r, lc, oc) = refs[23:]
    D, H2W, F2, NB = s.D, s.H2W, s.F2, s.NB
    QW = 3 * H2W
    FC, NFC = s.FC, F2 // s.FC
    C_OUT = QW

    def c_up(fc):
        return QW + H2W + 2 * FC * fc

    def c_dn(fc):
        return QW + H2W + 2 * FC * fc + FC

    d = lax.axis_index("dp")
    t = lax.axis_index("tensor")
    g = d // s.sub
    z = g // YX
    yx = g % YX
    rest = d % s.sub
    b2 = 2 - t
    b3 = 1 + t

    def at(zz, q):
        return ((zz * YX + q) * s.sub + rest, t)

    def flip(q, bit):
        y_bit, x_bit = q // 2, q % 2
        return jnp.where(bit == 2, (1 - y_bit) * 2 + x_bit, y_bit * 2 + 1 - x_bit)

    yx2 = flip(yx, b2)
    yx3 = flip(yx, b3)
    yx23 = 3 - yx
    pair = (d, 1 - t)
    peer2 = at(z, yx2)
    peer3 = at(z, yx3)
    zpeers = [at((z + k) % Z, yx) for k in range(1, Z)]

    barrier = pltpu.get_barrier_semaphore()
    for who in [pair, peer2, peer3] + zpeers:
        pl.semaphore_signal(barrier, inc=1, device_id=who, device_id_type=MESH)

    fetches = []

    def fetch(src, dst):
        cp = pltpu.make_async_copy(src, dst, lc.at[len(fetches)])
        cp.start()
        fetches.append(cp)

    own = W.at[t, z, yx]
    for j in range(3):
        for pr in range(2):
            fetch(s_qkv.at[j, :, pl.ds(128 * pr, 128)], own.at[:, pl.ds(384 * pr + 128 * j, 128)])
    fetch(s_out, own.at[:, pl.ds(C_OUT, H2W)])
    for fc in range(NFC):
        fetch(s_up.at[:, pl.ds(fc * FC, FC)], own.at[:, pl.ds(c_up(fc), FC)])
        fetch(s_dn.at[:, pl.ds(fc * FC, FC)], own.at[:, pl.ds(c_dn(fc), FC)])
    n_shards = len(fetches)
    fetch(tok_in, tok)
    fetch(cot_in, cot)
    BUP[t] = jnp.broadcast_to(bup_own[...], (8, F2))

    half_rows = iota((8, BLK), 0)
    for b in range(NB):
        line = span[pl.ds(t * NB + b, 1), :]
        belongs = jnp.logical_and(half_rows // NB == line, half_rows % NB == b)
        M8[:, b * BLK:(b + 1) * BLK] = belongs.astype(F32)
    SPC[...] = jnp.concatenate([span[...].astype(F32), jnp.zeros((120, BLK), F32)], axis=0).T
    zeros_in = (span[...] == 0).astype(F32)
    ones_in = (span[...] == 1).astype(F32)
    n_zero = jnp.sum(zeros_in, axis=1, keepdims=True)
    n_one = jnp.sum(ones_in, axis=1, keepdims=True)
    counts = jnp.concatenate(
        [n_zero[:NB], n_one[:NB], n_zero[NB:2 * NB], n_one[NB:2 * NB]], axis=0
    )
    log_counts = jnp.log(counts)
    own_counts = jnp.sum(M8[...], axis=1, keepdims=True)
    code = iota((16, 1), 0)
    block_of = (code // 8) * NB + code % NB

    for cp in fetches[:n_shards]:
        cp.wait()
    pl.semaphore_wait(barrier, 3 + Z - 1)

    def remote(src, dst, ss, rs, who):
        return pltpu.make_async_remote_copy(
            src_ref=src, dst_ref=dst, send_sem=ss, recv_sem=rs, device_id=who, device_id_type=MESH
        )

    chunks = s.ag_chunks
    group_of = {"o": yx, "2": yx2, "3": yx3, "23": yx23}
    kinds = ["z1", "z2", "z3"] + [a + str(k) for a in ("2s", "3s", "3t") for k in range(Z)]
    kinds += ["2g", "3g", "3h"] + ["p" + a for a in group_of]
    number = {kind: i for i, kind in enumerate(kinds)}

    def ag_copy(c, kind, got=False):
        lo, n = chunks[c]
        cols = pl.ds(lo, n)
        if kind[0] == "z":
            k = int(kind[1])
            window, who = W.at[t, (z + Z - k) % Z if got else z, yx, :, cols], zpeers[k - 1]
        elif kind[0] == "p":
            window, who = W.at[1 - t if got else t, :, group_of[kind[1:]], :, cols], pair
        else:
            there, here, who = {
                "2s": (yx2, yx, peer2), "3s": (yx3, yx, peer3), "3t": (yx23, yx2, peer3),
                "2g": (yx2, yx, peer2), "3g": (yx3, yx, peer3), "3h": (yx23, yx2, peer3),
            }[kind[:2]]
            group = there if got else here
            if len(kind) == 2:
                window = W.at[t, :, group, :, cols]
            else:
                window = W.at[t, (z + Z - int(kind[2])) % Z, group, :, cols]
        i = number[kind]
        return remote(window, window, ag_s.at[c, i], ag_r.at[c, i], who)

    def ag_done(place):
        for c in s.need[place]:
            for name in group_of:
                ag_copy(c, "p" + name, True).wait_recv()

    order = (1, 3, 2)
    after = (0, 1, 3, 2)

    def ag_events(fine):
        if not fine:
            return [
                ([], ["z1", "z3", "z2"]),
                (["z1", "z3", "z2"], ["2g", "3g", "po"]),
                (["2g"], ["3h", "p2"]),
                (["3g"], ["p3"]),
                (["3h"], ["p23"]),
            ]
        out = [([], ["z1", "z3", "z2", "2s0", "3s0"])]
        out += [([f"z{k}"], [f"2s{k}", f"3s{k}"] + (["po"] if k == 2 else [])) for k in order]
        out += [([f"2s{k}"], [f"3t{k}"] + (["p2"] if k == 2 else [])) for k in after]
        out += [([f"3s{k}" for k in after], ["p3"]), ([f"3t{k}" for k in after], ["p23"])]
        return out

    gathers = [ag_events(fine) for fine in s.ag_fine]

    def ag_event(c, step):
        arrived, starts = gathers[c][step]
        for kind in arrived:
            ag_copy(c, kind, True).wait_recv()
        for kind in starts:
            ag_copy(c, kind).start()

    def run(events):
        for kind, c, step in events:
            if kind == "a":
                ag_event(c, step)
            elif kind == "r":
                rs_steps[step](c)
            else:
                small_step(step)

    def in_slots(i, places):
        for when, events in enumerate(places):
            if events:
                @pl.when(i == when)
                def _():
                    run(events)

    def small_copy(i, src, dst, who):
        return remote(src, dst, sx_s.at[i], sx_r.at[i], who)

    def exchange(i, who):
        return small_copy(5 + i, SM.at[i], SMR.at[i], who)

    def small_step(i):
        whos = (pair, peer3, peer2)
        if i > 0:
            exchange(i - 1, whos[i - 1]).wait_recv()
            SM[i] = SM[i - 1] + SMR[i - 1]
        if i < 3:
            exchange(i, whos[i]).start()
        else:
            SMR[3 + z] = SM[3]
            for k in range(1, Z):
                small_copy(7 + k, SM.at[3], SMR.at[3 + z], zpeers[k - 1]).start()

    run(s.plan["first"])
    bup_copy = small_copy(0, BUP.at[t], BUP.at[t], pair)
    bup_copy.start()

    def wl(half, lo, n):
        return W[half, :, :, :, pl.ds(lo, n)].reshape(D, n)

    def rows_of(b, n=BLK):
        return pl.ds(pl.multiple_of(b * n, n), n)

    def loop(count, body, places=()):
        def step(i, _):
            body(i)
            in_slots(i, places)
            return 0

        lax.fori_loop(0, count, step, 0)


    for cp in fetches[n_shards:]:
        cp.wait()

    def norm_one(b, _):
        r = rows_of(b)
        unit, _inv = unit_rows(tok[r, :].astype(F32))
        low = (unit * gain1[...]).astype(BF)
        H1[r, :] = low
        H1T[:, r] = low.T
        COTT[:, r] = cot[r, :].T
        return 0

    lax.fori_loop(0, NB, norm_one, 0)

    BUACC[...] = jnp.zeros_like(BUACC)
    ACC[...] = jnp.zeros_like(ACC)
    DSV[...] = jnp.zeros_like(DSV)

    q_scale = jnp.where(iota((1, 384), 1) < 128, 1.0 / math.sqrt(HD), 1.0).astype(F32)
    member_low = jnp.concatenate([M8[...], M8[...]], axis=0).astype(BF)

    def ksv_copy(pr, got=False):
        window = KSV.at[pr, 1 - t if got else t]
        return small_copy(1 + pr, window, window, pair)

    def project(pr):
        lo = 384 * pr
        for half in range(2):
            QKV[half, :, lo:lo + 384] = (nn(H1[...], wl(half, lo, 384)) * q_scale).astype(BF)
        for half in range(2):
            sums = nn(member_low, QKV[half, :, lo + 128:lo + 384])[:8]
            KSV[pr, t, :, 256 * half:256 * half + 256] = (sums / own_counts).astype(BF).astype(F32)
        ksv_copy(pr).start()

    run(s.plan["second"])
    ag_done("second")
    project(0)
    run(s.plan["mid"])
    ag_done("mid")
    project(1)
    run(s.plan["third"])
    for pr in range(2):
        ksv_copy(pr, True).wait_recv()
        everything = KSV[pr].reshape(16, 512).astype(BF)
        for half in range(2):
            KSB[half, pr] = everything[:, 256 * half:256 * half + 128]
            VSB[half, pr] = everything[:, 256 * half + 128:256 * half + 256]

    even = iota((BLK, 128), 1) < HD

    def stacked(values):
        zero = jnp.zeros_like(values)
        return jnp.concatenate([jnp.where(even, values, zero), jnp.where(even, zero, values)], axis=0)

    def beside(values):
        return jnp.concatenate([values[:HD, :BLK], values[HD:, BLK:]], axis=0).astype(BF).T

    def part_of(half, pr, r, which):
        lo = 384 * pr + 128 * which
        return QKV[half, r, lo:lo + 128]

    def keys_of(half, pr, r):
        return jnp.concatenate([part_of(half, pr, r, 1), KSB[half, pr]], axis=0)

    def values_of(half, pr, r):
        return jnp.concatenate([part_of(half, pr, r, 2), VSB[half, pr]], axis=0)

    units = [(half, pr) for half in range(2) for pr in range(2)]

    def attend(b):
        r = rows_of(b)
        seen = block_of < t * NB + b
        scores = [nt(keys_of(half, pr, r), stacked(part_of(half, pr, r, 0))) for half, pr in units]
        probs = []
        for (half, pr), score in zip(units, scores):
            near = score[:BLK]
            far = jnp.where(seen, score[BLK:] + log_counts, MASKED)
            largest = jnp.maximum(jnp.max(near, axis=0, keepdims=True), jnp.max(far, axis=0, keepdims=True))
            near = jnp.exp(near - largest)
            far = jnp.exp(far - largest)
            inv = 1.0 / (jnp.sum(near, axis=0, keepdims=True) + jnp.sum(far, axis=0, keepdims=True))
            low = jnp.concatenate([(near * inv).astype(BF), (far * inv).astype(BF)], axis=0)
            PT[half, b, pr] = low
            probs.append(low)
        for (half, pr), low in zip(units, probs):
            O[half, r, 128 * pr:128 * pr + 128] = beside(tn(values_of(half, pr, r), low))

    loop(NB, attend, s.plan["attend"])

    run(s.plan["proj_wait"])
    ag_done("proj_wait")
    small_copy(0, BUP.at[1 - t], BUP.at[1 - t], pair).wait_recv()

    def out_proj(i):
        r = rows_of(i, s.big["proj"])
        branch = nt(O[0, r, :], wl(0, C_OUT, H2W)) + nt(O[1, r, :], wl(1, C_OUT, H2W))
        middle = tok[r, :].astype(F32) + (branch + bout[...])
        RES[r, :] = middle
        unit, _inv = unit_rows(middle)
        low = (unit * gain2[...]).astype(BF)
        H2[r, :] = low
        H2T[:, r] = low.T

    loop(s.rows // s.big["proj"], out_proj, s.plan["proj"])

    c0 = math.sqrt(2.0 / math.pi)
    c1 = c0 * 0.044715

    def feed(fc):
        cols = slice(fc * FC, (fc + 1) * FC)

        def one(i):
            r = rows_of(i, s.big["feed"])
            for half in range(2):
                x = nn(H2[r, :], wl(half, c_up(fc), FC)) + BUP[half, 0:1, cols]
                gh = nn(cot[r, :], wl(half, c_dn(fc), FC))
                sq = x * x
                th = jnp.tanh(x * (c0 + c1 * sq))
                up = 0.5 + 0.5 * th
                HID[half, r, cols] = (x * up).astype(BF)
                slope = up + (0.5 * x) * (1.0 - th * th) * (c0 + (3.0 * c1) * sq)
                gi = gh * slope
                GI[half, r, cols] = gi.astype(BF)
                BUACC[half, :, cols] += eight(gi)

        loop(s.rows // s.big["feed"], one, s.plan["feed" + str(fc)])

    def over_units(values, r, place):
        total = None
        for half in range(2):
            for fc in range(NFC):
                part = nt(values[half, r, fc * FC:(fc + 1) * FC], wl(half, place(fc), FC))
                total = part if total is None else total + part
        return total

    def feed_back(i):
        r = rows_of(i, s.big["feed_back"])
        g2 = over_units(GI, r, c_up)
        unit, inverse = unit_rows(RES[r, :])
        e = g2 * gain2[...]
        m1 = jnp.mean(e, axis=-1, keepdims=True)
        m2 = jnp.mean(e * unit, axis=-1, keepdims=True)
        grad_out = cot[r, :].astype(F32)
        mid = grad_out + inverse * (e - m1 - unit * m2)
        MID[r, :] = mid
        low = mid.astype(BF)
        GB[r, :] = low
        GBT[:, r] = low.T
        for half in range(2):
            GO[half, r, :] = nn(low, wl(half, C_OUT, H2W)).astype(BF)
        ACC[1] += eight(g2 * unit)
        ACC[2] += eight(mid)
        ACC[3] += eight(grad_out)

    def give(i):
        r = rows_of(i, s.big["give"])
        H1[r, :] = (RES[r, :] + (over_units(HID, r, c_dn) + bdown[...])).astype(BF)

    rchunks = s.rs_chunks

    def rs_copy(c, kind):
        lo, n = rchunks[c]
        cols = pl.ds(lo, n)
        if kind == 0:
            src, dst, who = G.at[1 - t, :, :, :, cols], R0.at[:, :, :, cols], pair
        elif kind == 1:
            src, dst, who = G.at[t, :, yx3, :, cols], R1.at[0, :, :, cols], peer3
        elif kind == 2:
            src, dst, who = G.at[t, :, yx23, :, cols], R1.at[1, :, :, cols], peer3
        elif kind == 3:
            src, dst, who = G.at[t, :, yx2, :, cols], R2.at[:, :, cols], peer2
        else:
            k = kind - 3
            src, dst, who = G.at[t, (z + k) % Z, yx, :, cols], R3.at[k - 1, :, cols], zpeers[k - 1]
        return remote(src, dst, rs_s.at[c, kind], rs_r.at[c, kind], who)

    def rs0(c):
        rs_copy(c, 0).start()

    def rs1(c):
        lo, n = rchunks[c]
        rs_copy(c, 0).wait_recv()
        cols = pl.ds(lo, n)

        def add(q):
            for zz in range(Z):
                G[t, zz, q, :, cols] = (
                    G[t, zz, q, :, cols].astype(F32) + R0[zz, q, :, cols].astype(F32)
                ).astype(BF)

        add(yx23)
        rs_copy(c, 2).start()
        add(yx3)
        rs_copy(c, 1).start()
        add(yx2)
        add(yx)

    def rs2(c):
        lo, n = rchunks[c]
        cols = pl.ds(lo, n)

        def add(q, j):
            for zz in range(Z):
                G[t, zz, q, :, cols] = (
                    G[t, zz, q, :, cols].astype(F32) + R1[j, zz, :, cols].astype(F32)
                ).astype(BF)

        rs_copy(c, 2).wait_recv()
        add(yx2, 1)
        rs_copy(c, 3).start()
        rs_copy(c, 1).wait_recv()
        add(yx, 0)

    def rs3(c):
        lo, n = rchunks[c]
        cols = pl.ds(lo, n)
        rs_copy(c, 3).wait_recv()
        for zz in range(Z):
            G[t, zz, yx, :, cols] = (
                G[t, zz, yx, :, cols].astype(F32) + R2[zz, :, cols].astype(F32)
            ).astype(BF)
        for kind in (4, 5, 6):
            rs_copy(c, kind).start()

    def rs4(c):
        lo, n = rchunks[c]
        cols = pl.ds(lo, n)
        total = G[t, z, yx, :, cols].astype(F32)
        for kind in (4, 5, 6):
            rs_copy(c, kind).wait_recv()
            total = total + R3[kind - 4, :, cols].astype(F32)
        total = total * s.factor
        if lo < QW:
            for piece in range(n // 128):
                pr, j = (lo // 128 + piece) // 3, (lo // 128 + piece) % 3
                g_qkv[j, :, 128 * pr:128 * pr + 128] = total[:, 128 * piece:128 * piece + 128]
        elif lo == C_OUT:
            g_out[...] = total
        else:
            for part in range(n // FC):
                place = (lo - QW - H2W) // FC + part
                dst = g_dn if place % 2 else g_up
                dst[:, (place // 2) * FC:(place // 2 + 1) * FC] = total[:, part * FC:(part + 1) * FC]

    rs_steps = (rs0, rs1, rs2, rs3, rs4)

    def weight_grad(lhs, rhs, lo, c_lo, n):
        for half in range(2):
            y = nn(lhs[...], rhs[half, :, lo:lo + n]).astype(BF)
            G[half, :, :, :, c_lo:c_lo + n] = y.reshape(Z, YX, D // GROUPS, n)

    for fc in range(NFC):
        run(s.plan["feed" + str(fc) + "_wait"])
        ag_done("feed" + str(fc) + "_wait")
        feed(fc)
        weight_grad(H2T, GI, fc * FC, c_up(fc), FC)
        run(s.plan["w" + str(2 * fc)])
        weight_grad(COTT, HID, fc * FC, c_dn(fc), FC)
        run(s.plan["w" + str(2 * fc + 1)])

    loop(s.rows // s.big["feed_back"], feed_back, s.plan["feed_back"])
    weight_grad(GBT, O, 0, C_OUT, H2W)
    run(s.plan["out"])

    GP = GI

    def attend_back(pr, i):
        places = [(b, half) for b in range(s.back) for half in range(2)]
        places = [(i * s.back + b, half) for b, half in places]
        grads = [stacked(GO[half, rows_of(b), 128 * pr:128 * pr + 128]) for b, half in places]
        dps = [nt(values_of(half, pr, rows_of(b)), up) for (b, half), up in zip(places, grads)]
        scores = []
        for (b, half), dp in zip(places, dps):
            p = PT[half, b, pr].astype(F32)
            corr = jnp.sum(p * dp, axis=0, keepdims=True)
            scores.append((p * (dp - corr)).astype(BF))
        lo = 384 * pr
        for (b, half), ds in zip(places, scores):
            r = rows_of(b)
            dk = nn(ds, stacked(part_of(half, pr, r, 0)))
            GP[half, r, lo + 128:lo + 256] = dk[:BLK].astype(BF)
            DSV[pr, :, :, 256 * half:256 * half + 128] += dk[BLK:].reshape(2, 8, 128)
        for (b, half), ds in zip(places, scores):
            r = rows_of(b)
            GP[half, r, lo:lo + 128] = beside(tn(keys_of(half, pr, r), ds) * (1.0 / math.sqrt(HD)))
        for (b, half), up in zip(places, grads):
            dv = nn(PT[half, b, pr], up)
            GP[half, rows_of(b), lo + 256:lo + 384] = dv[:BLK].astype(BF)
            DSV[pr, :, :, 256 * half + 128:256 * half + 256] += dv[BLK:].reshape(2, 8, 128)

    span_lane = iota((BLK, 128), 1)

    def dsv_copy(pr):
        return small_copy(3 + pr, DSV.at[pr, 1 - t], DSVR.at[pr], pair)

    def shared(pr):
        dsv_copy(pr).wait_recv()
        SHARE[pr] = (DSV[pr, t] + DSVR[pr]) / own_counts
        lo = 384 * pr

        def spread(b):
            r = rows_of(b)
            column = jnp.sum(jnp.where(span_lane == t * NB + b, SPC[...], 0.0), axis=1, keepdims=True)
            first = column == 0.0
            for half in range(2):
                lanes = slice(256 * half, 256 * half + 256)
                add = jnp.where(first, SHARE[pr, pl.ds(b, 1), lanes], SHARE[pr, pl.ds(NB + b, 1), lanes])
                GP[half, r, lo + 128:lo + 384] = (GP[half, r, lo + 128:lo + 384].astype(F32) + add).astype(BF)

        loop(NB, spread)

    loop(NB // s.back, functools.partial(attend_back, 0), s.plan["back0"])
    dsv_copy(0).start()
    run(s.plan["share0"])
    shared(0)
    weight_grad(H1T, GP, 0, 0, 384)
    run(s.plan["q0"])
    loop(NB // s.back, functools.partial(attend_back, 1), s.plan["back1"])
    dsv_copy(1).start()
    weight_grad(H1T, GP, 384, 384, 128)
    run(s.plan["share1"])
    shared(1)
    weight_grad(H1T, GP, 512, 512, 256)
    run(s.plan["q1"])

    def last(i):
        r = rows_of(i, s.big["last"])
        grad = nt(GP[0, r, 0:QW], wl(0, 0, QW)) + nt(GP[1, r, 0:QW], wl(1, 0, QW))
        unit, inverse = unit_rows(tok[r, :].astype(F32))
        e = grad * gain1[...]
        m1 = jnp.mean(e, axis=-1, keepdims=True)
        m2 = jnp.mean(e * unit, axis=-1, keepdims=True)
        H2[r, :] = (MID[r, :] + inverse * (e - m1 - unit * m2)).astype(BF)
        ACC[0] += eight(grad * unit)

    loop(s.rows // s.big["last"], last, s.plan["last"])
    out_copies = [pltpu.make_async_copy(H2, dtok_out, oc.at[0]), pltpu.make_async_copy(H1, res_out, oc.at[1])]
    out_copies[0].start()

    folded = [jnp.sum(ACC[j], axis=0, keepdims=True) for j in range(4)]
    for half in range(2):
        line = jnp.sum(BUACC[half], axis=0, keepdims=True)
        folded += [line[:, j * D:(j + 1) * D] for j in range(F2 // D)]
    SM[0] = jnp.concatenate(folded, axis=0)

    run(s.plan["small"])
    loop(s.rows // s.big["give"], give, s.plan["give"])
    out_copies[1].start()
    run(s.plan["end"])
    for k in range(1, Z):
        small_copy(7 + k, SM.at[3], SMR.at[3 + (z + Z - k) % Z], zpeers[k - 1]).wait_recv()
    summed = (SMR[3] + SMR[4] + SMR[5] + SMR[6]) * s.factor
    o_gain1[...] = summed[0:1]
    o_gain2[...] = summed[1:2]
    o_bout[...] = summed[2:3]
    o_bdown[...] = summed[3:4]
    for j in range(2 * F2 // D):
        o_bup[:, j * D:(j + 1) * D] = summed[4 + j:5 + j]


    for cp in out_copies:
        cp.wait()
    for c in range(len(chunks)):
        for _arrived, starts in gathers[c]:
            for kind in starts:
                ag_copy(c, kind).wait_send()
    for c in range(len(rchunks)):
        for kind in range(7):
            rs_copy(c, kind).wait_send()
    bup_copy.wait_send()
    for pr in range(2):
        ksv_copy(pr).wait_send()
        dsv_copy(pr).wait_send()
    for i, who in enumerate((pair, peer3, peer2)):
        exchange(i, who).wait_send()
    for k in range(1, Z):
        small_copy(7 + k, SM.at[3], SMR.at[3 + z], zpeers[k - 1]).wait_send()


def deliver(n, *refs):
    ins, outs, held, (got, sent) = refs[:n], refs[n:2 * n], refs[2 * n:3 * n], refs[3 * n:]
    firsts = [pltpu.make_async_copy(ins[i], held[i], got.at[i]) for i in range(n)]
    seconds = [pltpu.make_async_copy(held[i], outs[i], sent.at[i]) for i in range(n)]
    for cp in firsts:
        cp.start()
    for first, second in zip(firsts, seconds):
        first.wait()
        second.start()
    for cp in seconds:
        cp.wait()


def shards(
    tokens, cotangent, span_ids, gain_one, w_qkv, w_out, b_out, gain_two, w_up, b_up, w_down, b_down
):
    s = Sizes()
    dp = lax.axis_size("dp")
    s.sub = dp // GROUPS
    s.D = tokens.shape[2]
    s.rows = tokens.shape[1]
    s.NB = s.rows // BLK
    s.H2W = w_qkv.shape[2]
    s.F2 = w_up.shape[1]
    s.factor = 1.0 / math.sqrt(dp * lax.axis_size("tensor") * s.rows)
    sub, D, H2W, F2, N, NB = s.sub, s.D, s.H2W, s.F2, s.rows, s.NB
    QW = 3 * H2W
    width = QW + H2W + 2 * F2
    s.FC = 512
    s.FC = 512
    s.big = {'proj': 512, 'feed': 512, 'feed_back': 512, 'last': 512, 'give': 512}
    s.back = 2
    s.ag_chunks = [(0, 384), (384, 384), (768, 1280), (2048, 1024)]
    s.ag_fine = (1, 1, 1, 1)
    s.need = {'second': (0,), 'mid': (1,), 'proj_wait': (2,), 'feed0_wait': (), 'feed1_wait': (3,)}
    s.rs_chunks = [(1024, 512), (1536, 512), (2048, 512), (2560, 512), (768, 256), (0, 384), (384, 128), (512, 256)]
    s.plan = {
        "first": (('a', 0, 0), ('a', 1, 0), ('a', 2, 0), ),
        "second": (('a', 0, 4), ('a', 1, 4), ('a', 0, 1), ('a', 0, 2), ('a', 2, 4), ('a', 0, 3), ('a', 1, 1), ('a', 1, 2), ('a', 0, 5), ('a', 0, 6), ('a', 1, 3), ('a', 0, 7), ('a', 3, 0), ('a', 0, 8), ('a', 2, 1), ('a', 1, 5), ('a', 1, 6), ('a', 1, 7), ('a', 2, 2), ('a', 1, 8), ('a', 0, 9), ('a', 3, 4), ),
        "mid": (('a', 2, 5), ('a', 2, 3), ('a', 1, 9), ('a', 3, 1), ('a', 2, 6), ('a', 3, 2), ),
        "third": (),
        "proj_wait": (('a', 2, 9), ('a', 3, 7), ('a', 3, 8), ),
        "feed0_wait": (),
        "feed1_wait": (),
        "w0": (('r', 0, 0), ),
        "w1": (('r', 1, 0), ),
        "w2": (('r', 2, 0), ),
        "w3": (('r', 3, 0), ),
        "out": (('r', 4, 0), ),
        "share0": (),
        "q0": (('r', 5, 0), ),
        "share1": (('r', 6, 0), ),
        "q1": (('r', 7, 0), ('r', 2, 3), ),
        "small": (('s', 0, 0), ),
        "end": (('r', 7, 2), ('r', 2, 4), ('r', 5, 3), ('s', 0, 2), ('r', 6, 3), ('r', 3, 4), ('r', 7, 3), ('s', 0, 3), ('r', 4, 4), ('r', 5, 4), ('r', 6, 4), ('r', 7, 4), ),
        "attend": (
            (('a', 2, 7), ('a', 3, 3), ),
            (('a', 2, 8), ('a', 3, 5), ),
            (),
            (('a', 3, 6), ),
        ),
        "proj": (
            (),
            (),
        ),
        "feed0": (
            (('a', 3, 9), ),
            (),
        ),
        "feed1": (
            (('r', 0, 1), ),
            (('r', 1, 1), ),
        ),
        "feed_back": (
            (('r', 0, 2), ('r', 2, 1), ),
            (('r', 3, 1), ('r', 1, 2), ),
        ),
        "back0": (
            (('r', 0, 3), ),
            (('r', 4, 1), ('r', 2, 2), ),
        ),
        "back1": (
            (('r', 3, 2), ),
            (('r', 1, 3), ('r', 5, 1), ('r', 0, 4), ('r', 4, 2), ),
        ),
        "last": (
            (('r', 6, 1), ('r', 3, 3), ),
            (('r', 7, 1), ('r', 5, 2), ),
        ),
        "give": (
            (('r', 4, 3), ),
            (('r', 1, 4), ('s', 0, 1), ('r', 6, 2), ),
        ),
    }
    groups = [[a * sub + b for b in range(sub)] for a in range(dp // sub)]
    pieces = [jnp.transpose(w_qkv, (1, 0, 2)), w_out.T, w_up, w_down.T]
    if sub > 1:
        pieces = [
            lax.all_gather(piece, "dp", axis=piece.ndim - 2, tiled=True, axis_index_groups=groups)
            for piece in pieces
        ]
    R = D // GROUPS

    def vm(*shape, dtype=BF):
        return pltpu.VMEM(shape, dtype)

    any_space = pl.BlockSpec(memory_space=pl.ANY)
    in_vmem = pl.BlockSpec(memory_space=pltpu.VMEM)
    results = (
        jax.ShapeDtypeStruct((N, D), BF),
        jax.ShapeDtypeStruct((N, D), BF),
        jax.ShapeDtypeStruct((3, R, H2W), F32),
        jax.ShapeDtypeStruct((R, H2W), F32),
        jax.ShapeDtypeStruct((R, F2), F32),
        jax.ShapeDtypeStruct((R, F2), F32),
        jax.ShapeDtypeStruct((1, D), F32),
        jax.ShapeDtypeStruct((1, D), F32),
        jax.ShapeDtypeStruct((1, D), F32),
        jax.ShapeDtypeStruct((1, D), F32),
        jax.ShapeDtypeStruct((1, 2 * F2), F32),
    )
    out = pl.pallas_call(
        functools.partial(kernel, s),
        out_shape=results,
        in_specs=[any_space] * 2 + [in_vmem] * 6 + [any_space] * 4,
        out_specs=[any_space] * 2 + [in_vmem] * 9,
        scratch_shapes=[
            vm(2, Z, YX, R, width),
            vm(2, Z, YX, R, width),
            vm(Z, YX, R, width),
            vm(2, Z, R, width),
            vm(Z, R, width),
            vm(Z - 1, R, width),
            vm(N, D),
            vm(D, N),
            vm(2, N, QW),
            vm(2, NB, 2, BLK + 16, 2 * BLK),
            vm(2, N, H2W),
            vm(N, D, dtype=F32),
            vm(N, D),
            vm(D, N),
            vm(D, N),
            vm(2, N, F2),
            vm(2, N, F2),
            vm(N, D),
            vm(D, N),
            vm(2, 8, F2, dtype=F32),
            vm(2, 2, 8, 512, dtype=F32),
            vm(2, 2, 16, 128),
            vm(2, 2, 16, 128),
            vm(2, 2, 8, 512, dtype=F32),
            vm(2, 8, 512, dtype=F32),
            vm(2, 8, 512, dtype=F32),
            vm(BLK, 128, dtype=F32),
            vm(8, N, dtype=F32),
            vm(2, 8, F2, dtype=F32),
            vm(4, 8, D, dtype=F32),
            vm(4, 8, D, dtype=F32),
            vm(7, 8, D, dtype=F32),
            vm(N, D),
            vm(N, D),
            vm(N, D, dtype=F32),
            vm(2, N, H2W),
            pltpu.SemaphoreType.DMA((len(s.ag_chunks), 22)),
            pltpu.SemaphoreType.DMA((len(s.ag_chunks), 22)),
            pltpu.SemaphoreType.DMA((len(s.rs_chunks), 7)),
            pltpu.SemaphoreType.DMA((len(s.rs_chunks), 7)),
            pltpu.SemaphoreType.DMA((11,)),
            pltpu.SemaphoreType.DMA((11,)),
            pltpu.SemaphoreType.DMA((16,)),
            pltpu.SemaphoreType.DMA((2,)),
        ],
        compiler_params=pltpu.CompilerParams(
            collective_id=0, has_side_effects=True, vmem_limit_bytes=62 << 20
        ),
    )(
        tokens[0], cotangent[0], span_ids[0], gain_one[None], gain_two[None], b_out[None], b_down[None],
        b_up[None], *pieces,
    )
    out = list(out)
    if sub > 1:
        for i in range(2, 6):
            out[i] = lax.psum_scatter(
                out[i], "dp", scatter_dimension=out[i].ndim - 2, tiled=True, axis_index_groups=groups
            )
        out[6:] = lax.psum(tuple(out[6:]), "dp", axis_index_groups=groups)
    else:
        out = pl.pallas_call(
            functools.partial(deliver, len(results)),
            out_shape=results,
            in_specs=[any_space] * len(results),
            out_specs=[any_space] * len(results),
            scratch_shapes=[pltpu.VMEM(r.shape, r.dtype) for r in results]
            + [pltpu.SemaphoreType.DMA((len(results),))] * 2,
        )(*out)
    result, d_tokens, dq, do, du, dd, g1, g2, bo, bd, bu = out
    return (
        result[None],
        d_tokens[None],
        g1[0],
        jnp.transpose(dq, (1, 0, 2)),
        do.T,
        bo[0],
        g2[0],
        du,
        bu[0],
        dd.T,
        bd[0],
    )


def solution(mesh):
    in_specs = (
        P("dp", "tensor", None),
        P("dp", "tensor", None),
        P("dp", None, None),
        P(),
        P("dp", None, "tensor"),
        P("tensor", "dp"),
        P(),
        P(),
        P("dp", "tensor"),
        P("tensor"),
        P("tensor", "dp"),
        P(),
    )
    out_specs = (
        P("dp", "tensor", None),
        P("dp", "tensor", None),
        P(),
        P("dp", None, "tensor"),
        P("tensor", "dp"),
        P(),
        P(),
        P("dp", "tensor"),
        P(),
        P("tensor", "dp"),
        P(),
    )
    return jax.shard_map(shards, mesh=mesh, in_specs=in_specs, out_specs=out_specs, check_vma=False)
```

time: 112 us -> 90.2 us (0.81)
  Pallas kernels: 111 us -> 89.2 us
    pallas_call x1, Pallas kernels: 109 us -> 86.3 us  [shards(): pl.pallas_call(functools.partial(kernel, s), out_shape=results, in_specs=...]
where the time goes in v3:
time: 90.2 us; the launch traced here: 90 us
  Pallas kernels  89.2 us (99%)
    pallas_call x1, Pallas kernels, shards(): pl.pallas_call(functools.partial(kernel, s), out_shape=results, in_specs=...  86.3 us
    pallas_call x1, Pallas kernels, shards(): pl.pallas_call(functools.partial(deliver, len(results)), out_shape=result...  2.87 us

profile of v3, /device:TPU:0, one launch (start us, length us, event | category | flops | bytes accessed | tf_op | source)
XLA Modules:
  0.0 90.0 jit_solution(13049994189618865968)
XLA Ops:
  0.6 86.3 %shard_map.203 = (bf16[1024,512]{1,0:T(8,128)(2,1)}, bf16[1024,512]{1,0:T(8,128)(2,1)}, f32[3,32,256]{2,1,0:T(8,128)}, f32[32,256]{1,0:T(8,128)}, f32[32,1024]{1...) custom-call(bf16[1024,512]{1,0:T(8,128)(2,1)} %bitcast.21, ...), custom_call_target="tpu_custom_call" | custom-call | tf_op jit(solution)/shard_map/pallas_call | solution.py:762
  87.0 2.9 %shard_map.204 = (bf16[1024,512]{1,0:T(8,128)(2,1)}, bf16[1024,512]{1,0:T(8,128)(2,1)}, f32[3,32,256]{2,1,0:T(8,128)}, f32[32,256]{1,0:T(8,128)}, f32[32,1024]{1...) custom-call(bf16[1024,512]{1,0:T(8,128)(2,1)} %get-tuple-element.33., ...), custom_call_target="tpu_custom_call" | custom-call | tf_op jit(solution)/shard_map/pallas_call | solution.py:828

commit v4 on v3

--- a/solution.py
+++ b/solution.py
@@ -56,10 +56,11 @@
 
 
 def kernel(s, *refs):
-    (tok_in, cot_in, span, gain1, gain2, bout, bdown, bup_own, s_qkv, s_out, s_up, s_dn) = refs[:12]
+    (tok_in, cot_in, span_in, gain1_in, gain2_in, bout_in, bdown_in, bup_in, s_qkv, s_out, s_up, s_dn) = refs[:12]
     (res_out, dtok_out, g_qkv, g_out, g_up, g_dn, o_gain1, o_gain2, o_bout, o_bdown, o_bup) = refs[12:23]
     (W, G, R0, R1, R2, R3, H1, H1T, QKV, PT, O, MID, H2, H2T, COTT, HID, GI, GB, GBT,
-     BUP, KSV, KSB, VSB, DSV, DSVR, SHARE, SPC, M8, BUACC, ACC, SM, SMR, tok, cot, RES, GO,
+     BUP, KSV, KSB, VSB, DSV, DSVR, SHARE, GAINS, SPC, M8, BUACC, ACC, SM, SMR, tok, cot, RES, GO,
+     span, gain1, gain2, bout, bdown, bup_own,
      ag_s, ag_r, rs_s, rs_r, sx_s, sx_r, lc, oc) = refs[23:]
     D, H2W, F2, NB = s.D, s.H2W, s.F2, s.NB
     QW = 3 * H2W
@@ -107,6 +108,8 @@
         cp.start()
         fetches.append(cp)
 
+    fetch(span_in, span)
+    fetch(bup_in, bup_own)
     own = W.at[t, z, yx]
     for j in range(3):
         for pr in range(2):
@@ -116,8 +119,12 @@
         fetch(s_up.at[:, pl.ds(fc * FC, FC)], own.at[:, pl.ds(c_up(fc), FC)])
         fetch(s_dn.at[:, pl.ds(fc * FC, FC)], own.at[:, pl.ds(c_dn(fc), FC)])
     n_shards = len(fetches)
+    for src, dst in ((gain1_in, gain1), (gain2_in, gain2), (bout_in, bout), (bdown_in, bdown)):
+        fetch(src, dst)
     fetch(tok_in, tok)
     fetch(cot_in, cot)
+    for cp in fetches[:2]:
+        cp.wait()
     BUP[t] = jnp.broadcast_to(bup_own[...], (8, F2))
 
     half_rows = iota((8, BLK), 0)
@@ -138,7 +145,7 @@
     code = iota((16, 1), 0)
     block_of = (code // 8) * NB + code % NB
 
-    for cp in fetches[:n_shards]:
+    for cp in fetches[2:n_shards]:
         cp.wait()
     pl.semaphore_wait(barrier, 3 + Z - 1)
 
@@ -275,6 +282,7 @@
 
     BUACC[...] = jnp.zeros_like(BUACC)
     ACC[...] = jnp.zeros_like(ACC)
+    GAINS[...] = jnp.zeros_like(GAINS)
     DSV[...] = jnp.zeros_like(DSV)
 
     q_scale = jnp.where(iota((1, 384), 1) < 128, 1.0 / math.sqrt(HD), 1.0).astype(F32)
@@ -498,17 +506,21 @@
         elif lo == C_OUT:
             g_out[...] = total
         else:
-            for part in range(n // FC):
-                place = (lo - QW - H2W) // FC + part
-                dst = g_dn if place % 2 else g_up
-                dst[:, (place // 2) * FC:(place // 2 + 1) * FC] = total[:, part * FC:(part + 1) * FC]
+            for piece in range(n // 128):
+                col = lo + 128 * piece - (QW + H2W)
+                dst = g_dn if (col // FC) % 2 else g_up
+                to = (col // (2 * FC)) * FC + col % FC
+                dst[:, to:to + 128] = total[:, 128 * piece:128 * piece + 128]
 
     rs_steps = (rs0, rs1, rs2, rs3, rs4)
 
     def weight_grad(lhs, rhs, lo, c_lo, n):
         for half in range(2):
-            y = nn(lhs[...], rhs[half, :, lo:lo + n]).astype(BF)
-            G[half, :, :, :, c_lo:c_lo + n] = y.reshape(Z, YX, D // GROUPS, n)
+            y = nn(lhs[...], rhs[half, :, lo:lo + n])
+            G[half, :, :, :, c_lo:c_lo + n] = y.astype(BF).reshape(Z, YX, D // GROUPS, n)
+            if c_lo < QW:
+                share = y * wl(half, c_lo, n).astype(F32)
+                GAINS[...] += sum(share[:, j:j + 128] for j in range(0, n, 128))
 
     for fc in range(NFC):
         run(s.plan["feed" + str(fc) + "_wait"])
@@ -584,6 +596,15 @@
     weight_grad(H1T, GP, 512, 512, 256)
     run(s.plan["q1"])
 
+    folded = [jnp.sum(GAINS[...].T, axis=0, keepdims=True) / gain1[...]]
+    folded += [jnp.sum(ACC[j], axis=0, keepdims=True) for j in range(1, 4)]
+    for half in range(2):
+        line = jnp.sum(BUACC[half], axis=0, keepdims=True)
+        folded += [line[:, j * D:(j + 1) * D] for j in range(F2 // D)]
+    SM[0] = jnp.concatenate(folded, axis=0)
+
+    run(s.plan["small"])
+
     def last(i):
         r = rows_of(i, s.big["last"])
         grad = nt(GP[0, r, 0:QW], wl(0, 0, QW)) + nt(GP[1, r, 0:QW], wl(1, 0, QW))
@@ -592,22 +613,27 @@
         m1 = jnp.mean(e, axis=-1, keepdims=True)
         m2 = jnp.mean(e * unit, axis=-1, keepdims=True)
         H2[r, :] = (MID[r, :] + inverse * (e - m1 - unit * m2)).astype(BF)
-        ACC[0] += eight(grad * unit)
 
     loop(s.rows // s.big["last"], last, s.plan["last"])
     out_copies = [pltpu.make_async_copy(H2, dtok_out, oc.at[0]), pltpu.make_async_copy(H1, res_out, oc.at[1])]
     out_copies[0].start()
 
-    folded = [jnp.sum(ACC[j], axis=0, keepdims=True) for j in range(4)]
-    for half in range(2):
-        line = jnp.sum(BUACC[half], axis=0, keepdims=True)
-        folded += [line[:, j * D:(j + 1) * D] for j in range(F2 // D)]
-    SM[0] = jnp.concatenate(folded, axis=0)
-
-    run(s.plan["small"])
     loop(s.rows // s.big["give"], give, s.plan["give"])
     out_copies[1].start()
-    run(s.plan["end"])
+    for c in range(len(chunks)):
+        for _arrived, starts in gathers[c]:
+            for kind in starts:
+                ag_copy(c, kind).wait_send()
+    bup_copy.wait_send()
+    for pr in range(2):
+        ksv_copy(pr).wait_send()
+        dsv_copy(pr).wait_send()
+    early = [e for e in s.plan["end"] if e[0] == "s" or e[2] < 4]
+    run(early)
+    for c in range(len(rchunks)):
+        for kind in range(4):
+            rs_copy(c, kind).wait_send()
+    run([e for e in s.plan["end"] if e not in early])
     for k in range(1, Z):
         small_copy(7 + k, SM.at[3], SMR.at[3 + (z + Z - k) % Z], zpeers[k - 1]).wait_recv()
     summed = (SMR[3] + SMR[4] + SMR[5] + SMR[6]) * s.factor
@@ -621,17 +647,9 @@
 
     for cp in out_copies:
         cp.wait()
-    for c in range(len(chunks)):
-        for _arrived, starts in gathers[c]:
-            for kind in starts:
-                ag_copy(c, kind).wait_send()
     for c in range(len(rchunks)):
-        for kind in range(7):
+        for kind in range(4, 7):
             rs_copy(c, kind).wait_send()
-    bup_copy.wait_send()
-    for pr in range(2):
-        ksv_copy(pr).wait_send()
-        dsv_copy(pr).wait_send()
     for i, who in enumerate((pair, peer3, peer2)):
         exchange(i, who).wait_send()
     for k in range(1, Z):
@@ -688,11 +706,11 @@
         "w3": (('r', 3, 0), ),
         "out": (('r', 4, 0), ),
         "share0": (),
-        "q0": (('r', 5, 0), ),
+        "q0": (('r', 5, 0), ('r', 2, 2), ),
         "share1": (('r', 6, 0), ),
-        "q1": (('r', 7, 0), ('r', 2, 3), ),
+        "q1": (('r', 7, 0), ('r', 4, 2), ),
         "small": (('s', 0, 0), ),
-        "end": (('r', 7, 2), ('r', 2, 4), ('r', 5, 3), ('s', 0, 2), ('r', 6, 3), ('r', 3, 4), ('r', 7, 3), ('s', 0, 3), ('r', 4, 4), ('r', 5, 4), ('r', 6, 4), ('r', 7, 4), ),
+        "end": (('r', 7, 2), ('s', 0, 2), ('r', 2, 4), ('r', 5, 3), ('r', 6, 3), ('r', 7, 3), ('s', 0, 3), ('r', 3, 4), ('r', 4, 4), ('r', 5, 4), ('r', 6, 4), ('r', 7, 4), ),
         "attend": (
             (('a', 2, 7), ('a', 3, 3), ),
             (('a', 2, 8), ('a', 3, 5), ),
@@ -716,20 +734,20 @@
             (('r', 3, 1), ('r', 1, 2), ),
         ),
         "back0": (
-            (('r', 0, 3), ),
-            (('r', 4, 1), ('r', 2, 2), ),
+            (),
+            (('r', 0, 3), ('r', 4, 1), ),
         ),
         "back1": (
-            (('r', 3, 2), ),
-            (('r', 1, 3), ('r', 5, 1), ('r', 0, 4), ('r', 4, 2), ),
+            (),
+            (('r', 3, 2), ('r', 5, 1), ('r', 1, 3), ),
         ),
         "last": (
-            (('r', 6, 1), ('r', 3, 3), ),
-            (('r', 7, 1), ('r', 5, 2), ),
+            (('r', 6, 1), ('r', 0, 4), ('r', 2, 3), ),
+            (('r', 3, 3), ('r', 7, 1), ('s', 0, 1), ),
         ),
         "give": (
-            (('r', 4, 3), ),
-            (('r', 1, 4), ('s', 0, 1), ('r', 6, 2), ),
+            (('r', 5, 2), ),
+            (('r', 1, 4), ('r', 4, 3), ('r', 6, 2), ),
         ),
     }
     groups = [[a * sub + b for b in range(sub)] for a in range(dp // sub)]
@@ -762,7 +780,7 @@
     out = pl.pallas_call(
         functools.partial(kernel, s),
         out_shape=results,
-        in_specs=[any_space] * 2 + [in_vmem] * 6 + [any_space] * 4,
+        in_specs=[any_space] * 12,
         out_specs=[any_space] * 2 + [in_vmem] * 9,
         scratch_shapes=[
             vm(2, Z, YX, R, width),
@@ -791,6 +809,7 @@
             vm(2, 2, 8, 512, dtype=F32),
             vm(2, 8, 512, dtype=F32),
             vm(2, 8, 512, dtype=F32),
+            vm(D, 128, dtype=F32),
             vm(BLK, 128, dtype=F32),
             vm(8, N, dtype=F32),
             vm(2, 8, F2, dtype=F32),
@@ -801,13 +820,19 @@
             vm(N, D),
             vm(N, D, dtype=F32),
             vm(2, N, H2W),
+            vm(2 * NB, BLK, dtype=jnp.int32),
+            vm(1, D, dtype=F32),
+            vm(1, D, dtype=F32),
+            vm(1, D, dtype=F32),
+            vm(1, D, dtype=F32),
+            vm(1, F2, dtype=F32),
             pltpu.SemaphoreType.DMA((len(s.ag_chunks), 22)),
             pltpu.SemaphoreType.DMA((len(s.ag_chunks), 22)),
             pltpu.SemaphoreType.DMA((len(s.rs_chunks), 7)),
             pltpu.SemaphoreType.DMA((len(s.rs_chunks), 7)),
             pltpu.SemaphoreType.DMA((11,)),
             pltpu.SemaphoreType.DMA((11,)),
-            pltpu.SemaphoreType.DMA((16,)),
+            pltpu.SemaphoreType.DMA((24,)),
             pltpu.SemaphoreType.DMA((2,)),
         ],
         compiler_params=pltpu.CompilerParams(

time: 90.2 us -> 88.5 us (0.981)
  Pallas kernels: 89.2 us -> 87.4 us
    pallas_call x1, Pallas kernels: 86.3 us -> 84.6 us  [shards(): pl.pallas_call(functools.partial(kernel, s), out_shape=results, in_specs=...]
where the time goes in v4:
time: 88.5 us; the launch traced here: 88.2 us
  Pallas kernels  87.4 us (99%)
    pallas_call x1, Pallas kernels, shards(): pl.pallas_call(functools.partial(kernel, s), out_shape=results, in_specs=...  84.6 us
    pallas_call x1, Pallas kernels, shards(): pl.pallas_call(functools.partial(deliver, len(results)), out_shape=result...  2.87 us

profile of v4, /device:TPU:0, one launch (start us, length us, event | category | flops | bytes accessed | tf_op | source)
XLA Modules:
  0.0 88.2 jit_solution(3362057961044225222)
XLA Ops:
  0.6 84.6 %shard_map.203 = (bf16[1024,512]{1,0:T(8,128)(2,1)}, bf16[1024,512]{1,0:T(8,128)(2,1)}, f32[3,32,256]{2,1,0:T(8,128)}, f32[32,256]{1,0:T(8,128)}, f32[32,1024]{1...) custom-call(bf16[1024,512]{1,0:T(8,128)(2,1)} %bitcast.21, ...), custom_call_target="tpu_custom_call" | custom-call | tf_op jit(solution)/shard_map/pallas_call | solution.py:780
  85.2 2.9 %shard_map.204 = (bf16[1024,512]{1,0:T(8,128)(2,1)}, bf16[1024,512]{1,0:T(8,128)(2,1)}, f32[3,32,256]{2,1,0:T(8,128)}, f32[32,256]{1,0:T(8,128)}, f32[32,1024]{1...) custom-call(bf16[1024,512]{1,0:T(8,128)(2,1)} %get-tuple-element.33., ...), custom_call_target="tpu_custom_call" | custom-call | tf_op jit(solution)/shard_map/pallas_call | solution.py:853

commit v5 on v4

--- a/solution.py
+++ b/solution.py
@@ -123,27 +123,6 @@
         fetch(src, dst)
     fetch(tok_in, tok)
     fetch(cot_in, cot)
-    for cp in fetches[:2]:
-        cp.wait()
-    BUP[t] = jnp.broadcast_to(bup_own[...], (8, F2))
-
-    half_rows = iota((8, BLK), 0)
-    for b in range(NB):
-        line = span[pl.ds(t * NB + b, 1), :]
-        belongs = jnp.logical_and(half_rows // NB == line, half_rows % NB == b)
-        M8[:, b * BLK:(b + 1) * BLK] = belongs.astype(F32)
-    SPC[...] = jnp.concatenate([span[...].astype(F32), jnp.zeros((120, BLK), F32)], axis=0).T
-    zeros_in = (span[...] == 0).astype(F32)
-    ones_in = (span[...] == 1).astype(F32)
-    n_zero = jnp.sum(zeros_in, axis=1, keepdims=True)
-    n_one = jnp.sum(ones_in, axis=1, keepdims=True)
-    counts = jnp.concatenate(
-        [n_zero[:NB], n_one[:NB], n_zero[NB:2 * NB], n_one[NB:2 * NB]], axis=0
-    )
-    log_counts = jnp.log(counts)
-    own_counts = jnp.sum(M8[...], axis=1, keepdims=True)
-    code = iota((16, 1), 0)
-    block_of = (code // 8) * NB + code % NB
 
     for cp in fetches[2:n_shards]:
         cp.wait()
@@ -248,6 +227,9 @@
                 small_copy(7 + k, SM.at[3], SMR.at[3 + z], zpeers[k - 1]).start()
 
     run(s.plan["first"])
+    for cp in fetches[:2]:
+        cp.wait()
+    BUP[t] = jnp.broadcast_to(bup_own[...], (8, F2))
     bup_copy = small_copy(0, BUP.at[t], BUP.at[t], pair)
     bup_copy.start()
 
@@ -279,6 +261,25 @@
         return 0
 
     lax.fori_loop(0, NB, norm_one, 0)
+
+    half_rows = iota((8, BLK), 0)
+    for b in range(NB):
+        line = span[pl.ds(t * NB + b, 1), :]
+        belongs = jnp.logical_and(half_rows // NB == line, half_rows % NB == b)
+        M8[:, b * BLK:(b + 1) * BLK] = belongs.astype(F32)
+    SPC[...] = jnp.concatenate([span[...].astype(F32), jnp.zeros((120, BLK), F32)], axis=0).T
+    zeros_in = (span[...] == 0).astype(F32)
+    ones_in = (span[...] == 1).astype(F32)
+    n_zero = jnp.sum(zeros_in, axis=1, keepdims=True)
+    n_one = jnp.sum(ones_in, axis=1, keepdims=True)
+    counts = jnp.concatenate(
+        [n_zero[:NB], n_one[:NB], n_zero[NB:2 * NB], n_one[NB:2 * NB]], axis=0
+    )
+    log_counts = jnp.log(counts)
+    own_counts = jnp.sum(M8[...], axis=1, keepdims=True)
+    code = iota((16, 1), 0)
+    block_of = (code // 8) * NB + code % NB
+
 
     BUACC[...] = jnp.zeros_like(BUACC)
     ACC[...] = jnp.zeros_like(ACC)
@@ -658,8 +659,18 @@
 
 def deliver(n, *refs):
     ins, outs, held, (got, sent) = refs[:n], refs[n:2 * n], refs[2 * n:3 * n], refs[3 * n:]
-    firsts = [pltpu.make_async_copy(ins[i], held[i], got.at[i]) for i in range(n)]
-    seconds = [pltpu.make_async_copy(held[i], outs[i], sent.at[i]) for i in range(n)]
+    pieces = []
+    for i in range(n):
+        rows = ins[i].shape[0]
+        cuts = 4 if rows >= 4 * BLK else 1
+        for j in range(cuts):
+            pieces.append((i, pl.ds(j * (rows // cuts), rows // cuts)))
+    firsts = [
+        pltpu.make_async_copy(ins[i].at[w], held[i].at[w], got.at[k]) for k, (i, w) in enumerate(pieces)
+    ]
+    seconds = [
+        pltpu.make_async_copy(held[i].at[w], outs[i].at[w], sent.at[k]) for k, (i, w) in enumerate(pieces)
+    ]
     for cp in firsts:
         cp.start()
     for first, second in zip(firsts, seconds):
@@ -856,7 +867,7 @@
             in_specs=[any_space] * len(results),
             out_specs=[any_space] * len(results),
             scratch_shapes=[pltpu.VMEM(r.shape, r.dtype) for r in results]
-            + [pltpu.SemaphoreType.DMA((len(results),))] * 2,
+            + [pltpu.SemaphoreType.DMA((len(results) + 6,))] * 2,
         )(*out)
     result, d_tokens, dq, do, du, dd, g1, g2, bo, bd, bu = out
     return (

time: 88.5 us -> 88.3 us (level)
  no operation moved by 1% of the time
where the time goes in v5:
time: 88.3 us; the launch traced here: 88.1 us
  Pallas kernels  87.3 us (99%)
    pallas_call x1, Pallas kernels, shards(): pl.pallas_call(functools.partial(kernel, s), out_shape=results, in_specs=...  84.6 us
    pallas_call x1, Pallas kernels, shards(): pl.pallas_call(functools.partial(deliver, len(results)), out_shape=result...  2.7 us

profile of v5, /device:TPU:0, one launch (start us, length us, event | category | flops | bytes accessed | tf_op | source)
XLA Modules:
  0.0 88.1 jit_solution(6871918393686798722)
XLA Ops:
  0.6 84.6 %shard_map.203 = (bf16[1024,512]{1,0:T(8,128)(2,1)}, bf16[1024,512]{1,0:T(8,128)(2,1)}, f32[3,32,256]{2,1,0:T(8,128)}, f32[32,256]{1,0:T(8,128)}, f32[32,1024]{1...) custom-call(bf16[1024,512]{1,0:T(8,128)(2,1)} %bitcast.21, ...), custom_call_target="tpu_custom_call" | custom-call | tf_op jit(solution)/shard_map/pallas_call | solution.py:791
  85.2 2.7 %shard_map.204 = (bf16[1024,512]{1,0:T(8,128)(2,1)}, bf16[1024,512]{1,0:T(8,128)(2,1)}, f32[3,32,256]{2,1,0:T(8,128)}, f32[32,256]{1,0:T(8,128)}, f32[32,1024]{1...) custom-call(bf16[1024,512]{1,0:T(8,128)(2,1)} %get-tuple-element.33., ...), custom_call_target="tpu_custom_call" | custom-call | tf_op jit(solution)/shard_map/pallas_call | solution.py:864
